TPU v7x, 32 devices: a whole 2x2x4 slice. The times are simulated.
32 devices in a mesh: dp: 8 (over z, y), tensor: 4 (over x, core).
Axes of the slice: x: 2, y: 2, z: 4, core: 2. Of those that a mesh axis runs over, the one named last changes fastest.
Arguments:
- tokens: bfloat16 [8224, 1024], P('dp', 'tensor'), may hold values from -6 to 6
- norm1_gain: float32 [1024], replicated, may hold values from 0.25 to 1.75
- norm1_bias: float32 [1024], replicated, may hold values from -3 to 3
- qkv_weight: bfloat16 [1024, 3072], P(None, 'tensor'), may hold values from -0.1875 to 0.1875
- query_bias: float32 [1024], P('tensor'), may hold values from -3 to 3
- value_bias: float32 [1024], P('tensor'), may hold values from -3 to 3
- out_weight: bfloat16 [1024, 1024], P('tensor'), may hold values from -1.5 to 1.5
- out_bias: float32 [1024], replicated, may hold values from -2 to 2
- layer_scale1: float32 [1024], replicated, may hold values from 0.25 to 2.5
- norm2_gain: float32 [1024], replicated, may hold values from 0.25 to 1.75
- norm2_bias: float32 [1024], replicated, may hold values from -3 to 3
- up_weight: bfloat16 [1024, 4096], P(None, 'tensor'), may hold values from -0.1875 to 0.1875
- up_bias: float32 [4096], P('tensor'), may hold values from -3 to 3
- down_weight: bfloat16 [4096, 1024], P('tensor'), may hold values from -0.09375 to 0.09375
- down_bias: float32 [1024], P('tensor'), may hold values from -2 to 2
- layer_scale2: float32 [1024], P('tensor'), may hold values from 0.25 to 2.5
- cotangent: bfloat16 [8224, 1024], P('dp', 'tensor'), may hold values from -6 to 6
Outputs:
- output: float32 [8224, 1024], P('dp', 'tensor')
- input_grad: float32 [8224, 1024], P('dp', 'tensor')
- grad_norm1_gain: float32 [1024], replicated
- grad_norm1_bias: float32 [1024], replicated
- grad_qkv_weight: float32 [1024, 3072], P(None, 'tensor')
- grad_query_bias: float32 [1024], P('tensor')
- grad_value_bias: float32 [1024], P('tensor')
- grad_out_weight: float32 [1024, 1024], P('tensor')
- grad_out_bias: float32 [1024], replicated
- grad_layer_scale1: float32 [1024], replicated
- grad_norm2_gain: float32 [1024], replicated
- grad_norm2_bias: float32 [1024], replicated
- grad_up_weight: float32 [1024, 4096], P(None, 'tensor')
- grad_up_bias: float32 [4096], P('tensor')
- grad_down_weight: float32 [4096, 1024], P('tensor')
- grad_down_bias: float32 [1024], P('tensor')
- grad_layer_scale2: float32 [1024], P('tensor')
All inputs are finite; a program needn't handle non-finite values.
Results may differ from a plain program's by a relative error of at most 0.02.
Values may be sent and summed in bfloat16 or wider, within the bound.
No kernel may reach another device: no remote copies, remote signals or barrier semaphores. Data moves between devices by JAX's collectives and lax.ppermute only.
A program may use at most 128 MiB of HBM per device.

v0:
```python
import math

import jax
import jax.numpy as jnp
from jax import lax
from jax.sharding import PartitionSpec as P

HD = 64
TOK_IMG = 257


EPS = 1e-06


def layer_norm(values, gain, bias):
    row_mean = jnp.mean(values, axis=-1, keepdims=True)
    centred = values - row_mean
    inv_std = lax.rsqrt(jnp.mean(centred * centred, axis=-1, keepdims=True) + EPS)
    normed = centred * inv_std
    return (normed, inv_std, normed * gain + bias)


def norm_back(upstream, normed, inv_std, gain):
    scaled = upstream * gain
    return inv_std * (
        scaled
        - jnp.mean(scaled, axis=-1, keepdims=True)
        - normed * jnp.mean(scaled * normed, axis=-1, keepdims=True)
    )


def gelu_parts(hidden_pre):
    cdf_value = 0.5 * (1.0 + jax.scipy.special.erf(hidden_pre * 2.0 ** (-0.5)))
    density = jnp.exp(-0.5 * hidden_pre * hidden_pre) * (2.0 * math.pi) ** (-0.5)
    return (hidden_pre * cdf_value, cdf_value + hidden_pre * density)


def contract_rows(left, right):
    return lax.dot_general(
        left, right, (((0,), (0,)), ((), ())), preferred_element_type=jnp.float32
    )


def contract_cols(left, right):
    return lax.dot_general(
        left, right, (((1,), (1,)), ((), ())), preferred_element_type=jnp.float32
    )


def score_probs(query_rows, key_rows, log_total):
    scores = jnp.einsum(
        "iqhd,ikhd->ihqk", query_rows, key_rows, preferred_element_type=jnp.float32
    ) * HD ** (-0.5)
    return jnp.exp(scores - log_total[..., None])


def shards(
    tokens,
    norm1_gain,
    norm1_bias,
    qkv_weight,
    query_bias,
    value_bias,
    out_weight,
    out_bias,
    layer_scale1,
    norm2_gain,
    norm2_bias,
    up_weight,
    up_bias,
    down_weight,
    down_bias,
    layer_scale2,
    cotangent,
):
    whole = lax.all_gather(tokens, "tensor", axis=1, tiled=True).astype(jnp.float32)
    row_count = whole.shape[0]
    images = row_count // TOK_IMG
    heads_local = qkv_weight.shape[1] // (3 * HD)
    shape_heads = (images, TOK_IMG, heads_local, HD)
    normed1, inv_std1, scaled1 = layer_norm(whole, norm1_gain, norm1_bias)
    lowered1 = scaled1.astype(jnp.bfloat16)
    projected = jnp.dot(lowered1, qkv_weight, preferred_element_type=jnp.float32).reshape(
        row_count, heads_local, 3, HD
    )
    query_rows = (
        (projected[:, :, 0] + query_bias.reshape(heads_local, HD))
        .astype(jnp.bfloat16)
        .reshape(shape_heads)
    )
    key_rows = projected[:, :, 1].astype(jnp.bfloat16).reshape(shape_heads)
    value_rows = (
        (projected[:, :, 2] + value_bias.reshape(heads_local, HD))
        .astype(jnp.bfloat16)
        .reshape(shape_heads)
    )
    scores = jnp.einsum(
        "iqhd,ikhd->ihqk", query_rows, key_rows, preferred_element_type=jnp.float32
    ) * HD ** (-0.5)
    log_total = jax.nn.logsumexp(scores, axis=-1)
    probs = jnp.exp(scores - log_total[..., None])
    mixed = (
        jnp.einsum(
            "ihqk,ikhd->iqhd",
            probs.astype(jnp.bfloat16),
            value_rows,
            preferred_element_type=jnp.float32,
        )
        .astype(jnp.bfloat16)
        .reshape(row_count, heads_local * HD)
    )
    attention_part = jnp.dot(mixed, out_weight, preferred_element_type=jnp.float32)
    attended = (
        lax.psum(attention_part.astype(jnp.bfloat16), "tensor").astype(jnp.float32) + out_bias
    )
    residual = whole + layer_scale1 * attended
    normed2, inv_std2, scaled2 = layer_norm(residual, norm2_gain, norm2_bias)
    lowered2 = scaled2.astype(jnp.bfloat16)
    hidden_pre = jnp.dot(lowered2, up_weight, preferred_element_type=jnp.float32) + up_bias
    activated, slope = gelu_parts(hidden_pre)
    activated_low = activated.astype(jnp.bfloat16)
    down_part = jnp.dot(activated_low, down_weight, preferred_element_type=jnp.float32)
    branch_cols = (
        lax.psum_scatter(
            down_part.astype(jnp.bfloat16), "tensor", scatter_dimension=1, tiled=True
        ).astype(jnp.float32)
        + down_bias
    )
    width_local = tokens.shape[1]
    col_start = lax.axis_index("tensor") * width_local
    residual_cols = lax.dynamic_slice_in_dim(residual, col_start, width_local, 1)
    output = residual_cols + layer_scale2 * branch_cols
    upstream_cols = cotangent.astype(jnp.float32)
    grad_layer_scale2 = jnp.sum(upstream_cols * branch_cols, axis=0)
    grad_down_bias = jnp.sum(upstream_cols * layer_scale2, axis=0)
    branch_grad_cols = (upstream_cols * layer_scale2).astype(jnp.bfloat16)
    branch_grad, upstream_low = (
        lax.all_gather(branch_grad_cols, "tensor", axis=1, tiled=True),
        lax.all_gather(cotangent, "tensor", axis=1, tiled=True),
    )
    upstream = upstream_low.astype(jnp.float32)
    grad_down_weight = contract_rows(activated_low, branch_grad)
    grad_hidden = contract_cols(branch_grad, down_weight)
    grad_pre = grad_hidden * slope
    grad_up_bias = jnp.sum(grad_pre, axis=0)
    grad_pre_low = grad_pre.astype(jnp.bfloat16)
    grad_up_weight = contract_rows(lowered2, grad_pre_low)
    grad_lowered2 = lax.psum(
        contract_cols(grad_pre_low, up_weight).astype(jnp.bfloat16), "tensor"
    ).astype(jnp.float32)
    grad_norm2_gain = jnp.sum(grad_lowered2 * normed2, axis=0)
    grad_norm2_bias = jnp.sum(grad_lowered2, axis=0)
    grad_residual = upstream + norm_back(grad_lowered2, normed2, inv_std2, norm2_gain)
    grad_layer_scale1 = jnp.sum(grad_residual * attended, axis=0)
    grad_out_bias = jnp.sum(grad_residual * layer_scale1, axis=0)
    grad_attended = (grad_residual * layer_scale1).astype(jnp.bfloat16)
    grad_out_weight = contract_rows(mixed, grad_attended)
    grad_mixed = contract_cols(grad_attended, out_weight).astype(jnp.bfloat16).reshape(shape_heads)
    probs_back = score_probs(query_rows, key_rows, log_total)
    grad_value = jnp.einsum(
        "ihqk,iqhd->ikhd",
        probs_back.astype(jnp.bfloat16),
        grad_mixed,
        preferred_element_type=jnp.float32,
    )
    grad_probs = jnp.einsum(
        "iqhd,ikhd->ihqk", grad_mixed, value_rows, preferred_element_type=jnp.float32
    )
    delta = jnp.sum(probs_back * grad_probs, axis=-1, keepdims=True)
    grad_scores = (probs_back * (grad_probs - delta) * HD ** (-0.5)).astype(jnp.bfloat16)
    grad_query = jnp.einsum(
        "ihqk,ikhd->iqhd", grad_scores, key_rows, preferred_element_type=jnp.float32
    )
    grad_key = jnp.einsum(
        "ihqk,iqhd->ikhd", grad_scores, query_rows, preferred_element_type=jnp.float32
    )
    grad_query_bias = jnp.sum(grad_query, axis=(0, 1)).reshape(heads_local * HD)
    grad_value_bias = jnp.sum(grad_value, axis=(0, 1)).reshape(heads_local * HD)
    grad_projected = (
        jnp.stack([grad_query, grad_key, grad_value], axis=3)
        .reshape(row_count, 3 * heads_local * HD)
        .astype(jnp.bfloat16)
    )
    grad_qkv_weight = contract_rows(lowered1, grad_projected)
    grad_lowered1 = lax.psum(
        contract_cols(grad_projected, qkv_weight).astype(jnp.bfloat16), "tensor"
    ).astype(jnp.float32)
    grad_norm1_gain = jnp.sum(grad_lowered1 * normed1, axis=0)
    grad_norm1_bias = jnp.sum(grad_lowered1, axis=0)
    grad_whole = grad_residual + norm_back(grad_lowered1, normed1, inv_std1, norm1_gain)
    input_grad = lax.dynamic_slice_in_dim(grad_whole, col_start, width_local, 1)
    (
        grad_norm1_gain,
        grad_norm1_bias,
        grad_qkv_weight,
        grad_query_bias,
        grad_value_bias,
        grad_out_weight,
        grad_out_bias,
        grad_layer_scale1,
        grad_norm2_gain,
        grad_norm2_bias,
        grad_up_weight,
        grad_up_bias,
        grad_down_weight,
        grad_down_bias,
        grad_layer_scale2,
    ) = lax.psum(
        (
            grad_norm1_gain,
            grad_norm1_bias,
            grad_qkv_weight,
            grad_query_bias,
            grad_value_bias,
            grad_out_weight,
            grad_out_bias,
            grad_layer_scale1,
            grad_norm2_gain,
            grad_norm2_bias,
            grad_up_weight,
            grad_up_bias,
            grad_down_weight,
            grad_down_bias,
            grad_layer_scale2,
        ),
        "dp",
    )
    return (
        output,
        input_grad,
        grad_norm1_gain,
        grad_norm1_bias,
        grad_qkv_weight,
        grad_query_bias,
        grad_value_bias,
        grad_out_weight,
        grad_out_bias,
        grad_layer_scale1,
        grad_norm2_gain,
        grad_norm2_bias,
        grad_up_weight,
        grad_up_bias,
        grad_down_weight,
        grad_down_bias,
        grad_layer_scale2,
    )


def solution(mesh):
    return jax.shard_map(
        shards,
        mesh=mesh,
        in_specs=(
            P("dp", "tensor"),
            P(),
            P(),
            P(None, "tensor"),
            P("tensor"),
            P("tensor"),
            P("tensor", None),
            P(),
            P(),
            P(),
            P(),
            P(None, "tensor"),
            P("tensor"),
            P("tensor", None),
            P("tensor"),
            P("tensor"),
            P("dp", "tensor"),
        ),
        out_specs=(
            P("dp", "tensor"),
            P("dp", "tensor"),
            P(),
            P(),
            P(None, "tensor"),
            P("tensor"),
            P("tensor"),
            P("tensor", None),
            P(),
            P(),
            P(),
            P(),
            P(None, "tensor"),
            P("tensor"),
            P("tensor", None),
            P("tensor"),
            P("tensor"),
        ),
        check_vma=False,
    )
```

profile of v0, /device:TPU:0, one launch (start us, length us, event | category | flops | bytes accessed | tf_op | source)
XLA Modules:
  0.0 811.1 jit_solution(14606177687387526413)
XLA Ops:
  9.5 25.7 %all-gather.4.cloned.1.call-done = bf16[1028,1024]{1,0:T(8,128)(2,1)} async-done(((bf16[1028,256]{1,0:T(8,128)(2,1)}), bf16[1028,1024]{1,0:T(8,128)(2,1)}) %all-gather.4.cloned.1.call-update) | async-done | bytes 2105360 | tf_op jit(solution)/shard_map/all_gather | solution.py:76
  44.8 3.6 squeeze.8
  65.6 51.9 %all-reduce.7.cloned.1.call-done = bf16[1028,1024]{1,0:T(8,128)(2,1)} async-done(((bf16[1028,1024]{1,0:T(8,128)(2,1)}), bf16[1028,1024]{1,0:T(8,128)(2,1)}) %all-reduce.7.cloned.1.call-update) | async-done | bytes 2105360 | tf_op jit(solution)/shard_map/psum | solution.py:114
  117.6 3.1 fusion.78
  121.6 5.1 multiply_convert_fusion.1
  128.0 3.7 convolution_convert_fusion.2
  131.8 31.7 %reduce-scatter.2.cloned.1.call-done = bf16[1028,256]{1,0:T(8,128)(2,1)} async-done(((bf16[1028,1024]{1,0:T(8,128)(2,1)}), bf16[1028,256]{1,0:T(8,128)(2,1)}) %reduce-scatter.2.cloned.1.call-update) | async-done | bytes 526352 | tf_op jit(solution)/shard_map/reduce_scatter | solution.py:124
  163.5 3.6 fusion.45
  167.1 23.0 %all-gather.8.cloned.1.call-done = bf16[1028,1024]{1,0:T(8,128)(2,1)} async-done(((bf16[1028,256]{1,0:T(8,128)(2,1)}), bf16[1028,1024]{1,0:T(8,128)(2,1)}) %all-gather.8.cloned.1.call-update) | async-done | bytes 2105360 | tf_op jit(solution)/shard_map/all_gather | solution.py:138
  190.2 6.4 fusion.82
  197.9 3.8 convolution_convert_fusion.1
  202.4 8.3 %fusion.48 = f32[1024,1024]{1,0:T(8,128)} fusion(bf16[1028,1024]{1,0:T(8,128)(2,1)} %copy-done.30, f32[1028,1024]{1,0:T(8,128)} %copy-done.3, f32[1024]{0:T(1024)} %param.27, f32[1024]{0:T(1024)S(1)} %copy-done.19, f32[1028]{0:T(1024)S(1)} %add_rsqrt_fusion, f32[1028]{0:T(1024)S(1)} %broadcast_multiply_fusion.4), kind=kOutput, calls=%fused_computation.81 | convolution fusion | flops 2161135616 | bytes 10526752 | tf_op jit(solution)/shard_map/dot_general | solution.py:39
  210.6 43.1 %all-reduce.9.cloned.1.call-done = bf16[1028,1024]{1,0:T(8,128)(2,1)} async-done(((bf16[1028,1024]{1,0:T(8,128)(2,1)}), bf16[1028,1024]{1,0:T(8,128)(2,1)}) %all-reduce.9.cloned.1.call-update) | async-done | bytes 2105360 | tf_op jit(solution)/shard_map/psum | solution.py:148
  253.7 4.6 fusion.18
  258.3 19.9 %all-gather.6.cloned.1.call-done = bf16[1028,1024]{1,0:T(8,128)(2,1)} async-done(((bf16[1028,256]{1,0:T(8,128)(2,1)}), bf16[1028,1024]{1,0:T(8,128)(2,1)}) %all-gather.6.cloned.1.call-update) | async-done | bytes 2105360 | tf_op jit(solution)/shard_map/all_gather | solution.py:139
  278.2 5.6 multiply_reduce_fusion.2
  287.8 5.1 bitcast_reduce_fusion
  292.9 4.0 fusion.54
  296.9 11.6 %fusion.39 = bf16[4,257,4,1,64]{1,4,2,0,3:T(8,128)(2,1)S(1)} fusion(f32[4,4,257,257]{2,3,1,0:T(8,128)} %fusion.54, f32[4,4,257,257]{2,3,1,0:T(8,128)} %copy-done.2, f32[4,4,257]{2,1,0:T(4,128)S(1)} %log_add_fusion, bf16[4,257,4,64]{1,0,3,2:T(4,128)(2,1)S(1)} %copy-done.11), kind=kOutput, calls=%fused_computation.70 | convolution fusion | flops 145046944 | bytes 9523392 | tf_op jit(solution)/shard_map/ihqk,iqhd->ikhd/dot_general | solution.py:174
  308.5 11.3 %bitcast_reduce_fusion.1 = (f32[4,64]{1,0:T(4,128)S(1)}, bf16[4,4,64,257]{3,2,1,0:T(8,128)(2,1)}) fusion(f32[4,4,257,257]{2,3,1,0:T(8,128)} %fusion.54, f32[4,4,257,257]{2,3,1,0:T(8,128)} %copy-done.2, f32[4,4,257]{2,1,0:T(4,128)S(1)} %log_add_fusion, bf16[4,257,4,64]{1,0,3,2:T(4,128)(2,1)S(1)} %copy-done.9), kind=kOutput, calls=%fused_computation.62 | convolution fusion | flops 145309856 | bytes 9524416 | tf_op jit(solution)/shard_map/ihqk,ikhd->iqhd/dot_general | solution.py:171
  321.6 3.2 copy.55
  324.8 4.1 convert_element_type.107
  328.9 4.9 convolution_convert_fusion
  333.9 7.2 fusion.83
  341.0 4.2 fusion.51
  345.2 4.7 fusion.62
  350.1 35.7 %all-reduce.11.cloned.1.call-done = bf16[1028,1024]{1,0:T(8,128)(2,1)} async-done(((bf16[1028,1024]{1,0:T(8,128)(2,1)}), bf16[1028,1024]{1,0:T(8,128)(2,1)}) %all-reduce.11.cloned.1.call-update) | async-done | bytes 2105360 | tf_op jit(solution)/shard_map/psum | solution.py:185
  385.8 7.0 fusion.19
  392.8 39.7 %all-reduce = (f32[1024]{0:T(1024)}, f32[1024]{0:T(1024)}, f32[256]{0:T(256)}, f32[256]{0:T(256)}, f32[1024]{0:T(1024)}, /*index=5*/f32[1024]{0:T(1024)}, f32[10...) all-reduce(f32[1024]{0:T(1024)S(1)} %get-tuple-element.19, ...), channel_id=1, replica_groups=mesh['dp'=8,'tensor'=4] {'dp'}, use_global_device_ids=true, to_apply=%region_16.0 | all-reduce | flops 8192 | bytes 65536 | tf_op jit(solution)/shard_map/psum | solution.py:208
  432.5 3.4 dynamic-slice_add_fusion
  435.9 357.6 %all-reduce.13.cloned.1.call-done = (f32[1024,768]{1,0:T(8,128)}, f32[256,1024]{1,0:T(8,128)}, f32[1024,1024]{1,0:T(8,128)}, f32[1024,1024]{1,0:T(8,128)}) async-done(((f32[1024,768]{1,0:T(8,128)}, f32[256,1024]{1,0:T(8,128)}, f32[1024,1024]{1,0:T(8,128)}, f32[1024,1024]{1,0:T(8,128)}), (f32[1024,768]{1,0:T(8,128)}, f32[256,1024]{1,0:T(8,128)}, f32[1024,1024]{1,0:T(8,128)}, ...) | async-done | bytes 12582928 | tf_op jit(solution)/shard_map/psum | solution.py:208
  793.5 3.9 copy.88
  (116 shorter events, 45.7 us)
Async XLA Ops:
  7.2 114.2 %copy-start = (bf16[1024,1024]{1,0:T(8,128)(2,1)S(1)}, bf16[1024,1024]{1,0:T(8,128)(2,1)}, u32[]{:S(2)}) copy-start(bf16[1024,1024]{1,0:T(8,128)(2,1)} %param.28) | copy-start | bytes 6291460
  7.2 32.5 %copy-start.20 = (f32[1024]{0:T(1024)S(1)}, f32[1024]{0:T(1024)}, u32[]{:S(2)}) copy-start(f32[1024]{0:T(1024)} %param.18) | copy-start | bytes 12292
  7.2 32.5 %copy-start.27 = (f32[1024]{0:T(1024)S(1)}, f32[1024]{0:T(1024)}, u32[]{:S(2)}) copy-start(f32[1024]{0:T(1024)} %param.19) | copy-start | bytes 12292
  7.2 28.0 %all-gather.4.cloned.1.call-start = ((), (), s32[]{:S(2)}) async-start(), calls=%async_computation.1 | async-start | bytes 2641920 | tf_op jit(solution)/shard_map/all_gather | solution.py:76
  8.0 109.6 %all-reduce.7.cloned.1.call-start = ((), (), s32[]{:S(2)}) async-start(), calls=%async_computation.2 | async-start | bytes 4227072 | tf_op jit(solution)/shard_map/psum | solution.py:114
  35.3 4.5 copy-start.5
  35.3 4.5 copy-start.24
  44.8 9.9 %copy-start.8 = (bf16[4,257,4,64]{1,0,3,2:T(4,128)(2,1)}, bf16[4,257,4,64]{1,0,3,2:T(4,128)(2,1)S(1)}, u32[]{:S(2)}) copy-start(bf16[4,257,4,64]{1,0,3,2:T(4,128)(2,1)S(1)} %convert_element_type.88) | copy-start | bytes 1579012
  54.7 3.0 copy-start.2
  54.7 2.6 copy-start.7
  62.4 55.2 %copy-start.17 = (f32[1024]{0:T(1024)S(1)}, f32[1024]{0:T(1024)}, u32[]{:S(2)}) copy-start(f32[1024]{0:T(1024)} %param.25) | copy-start | bytes 12292
  62.4 55.1 %copy-start.18 = (f32[1024]{0:T(1024)S(1)}, f32[1024]{0:T(1024)}, u32[]{:S(2)}) copy-start(f32[1024]{0:T(1024)} %param.24) | copy-start | bytes 12292
  65.6 97.9 %reduce-scatter.2.cloned.1.call-start = ((), (), s32[]{:S(2)}) async-start(), calls=%async_computation.3 | async-start | bytes 2641920 | tf_op jit(solution)/shard_map/reduce_scatter | solution.py:124
  120.7 5.9 copy-start.3
  121.6 6.4 copy-start.23
  128.0 35.5 %copy-start.22 = (f32[256]{0:T(256)S(1)}, f32[256]{0:T(256)}, u32[]{:S(2)}) copy-start(f32[256]{0:T(256)} %param.31) | copy-start | bytes 3076
  131.7 58.5 %all-gather.8.cloned.1.call-start = ((), (), s32[]{:S(2)}) async-start(), calls=%async_computation.5 | async-start | bytes 2641920 | tf_op jit(solution)/shard_map/all_gather | solution.py:138
  167.1 86.6 %all-reduce.9.cloned.1.call-start = ((), (), s32[]{:S(2)}) async-start(), calls=%async_computation.6 | async-start | bytes 4227072 | tf_op jit(solution)/shard_map/psum | solution.py:148
  201.7 76.4 %all-gather.6.cloned.1.call-start = ((), (), s32[]{:S(2)}) async-start(), calls=%async_computation.4 | async-start | bytes 2641920 | tf_op jit(solution)/shard_map/all_gather | solution.py:139
  202.3 183.5 %all-reduce.11.cloned.1.call-start = ((), (), s32[]{:S(2)}) async-start(), calls=%async_computation.7 | async-start | bytes 4227072 | tf_op jit(solution)/shard_map/psum | solution.py:185
  278.2 7.6 copy-start.15
  292.9 4.0 copy-start.11
  296.9 11.6 %copy-start.9 = (bf16[4,257,4,64]{1,0,3,2:T(4,128)(2,1)S(1)}, bf16[4,257,4,64]{1,0,3,2:T(4,128)(2,1)}, u32[]{:S(2)}) copy-start(bf16[4,257,4,64]{1,0,3,2:T(4,128)(2,1)} %copy-done.8) | copy-start | bytes 1579012
  308.5 11.3 %copy-start.14 = (bf16[4,4,64,257]{3,2,1,0:T(8,128)(2,1)S(1)}, bf16[4,4,64,257]{3,2,1,0:T(8,128)(2,1)}, u32[]{:S(2)}) copy-start(bf16[4,4,64,257]{3,2,1,0:T(8,128)(2,1)} %get-tuple-element.60) | copy-start | bytes 1579012
  333.8 459.7 %all-reduce.13.cloned.1.call-start = ((), (), s32[]{:S(2)}) async-start(), calls=%async_computation.8 | async-start | bytes 25165824 | tf_op jit(solution)/shard_map/psum | solution.py:208
  341.0 4.2 copy-start.6
  341.0 4.2 copy-start.28
  350.1 42.7 %copy-start.21 = (f32[256]{0:T(256)S(1)}, f32[256]{0:T(256)}, u32[]{:S(2)}) copy-start(f32[256]{0:T(256)} %get-tuple-element.28) | copy-start | bytes 3076
  793.5 3.9 copy-start.16
  793.5 4.9 copy-start.13
  798.4 3.7 copy-start.12
  798.4 5.7 copy-start.1
  (7 other events, 8.3 us)
Sparse Core Ops, SparseCore 0:
  9.6 25.6 all-gather.3
  65.7 51.8 all-reduce.6
  131.8 31.5 reduce-scatter.1
  167.2 22.9 all-gather.7
  201.9 51.8 all-reduce.8
  255.2 22.9 all-gather.5
  333.9 51.8 all-reduce.10
  392.4 401.0 all-reduce.12
where the time goes:
time: 816 us; the launch traced here: 811 us
  waiting for transfers between devices  590 us (72%)
  matrix products  89.5 us (11%)
  local copies, waits for them, and re-layouts  40.7 us (5%)
  blocking collectives  39.7 us (5%)
  other arithmetic  36.2 us (4%)
  between operations  14.7 us (2%)
    psum x1, waiting for transfers between devices, shards(): lax.psum((grad_norm1_gain, grad_norm1_bias, grad_qkv_weight, grad_query_b...  358 us
    psum x1, waiting for transfers between devices, shards(): lax.psum(attention_part.astype(jnp.bfloat16), 'tensor').astype(jnp.float32)  51.9 us
    psum x1, waiting for transfers between devices, shards(): lax.psum(contract_cols(grad_pre_low, up_weight).astype(jnp.bfloat16), 'te...  43.1 us
    psum x1, blocking collectives, shards(): lax.psum((grad_norm1_gain, grad_norm1_bias, grad_qkv_weight, grad_query_b...  39.7 us
    psum x1, waiting for transfers between devices, shards(): lax.psum(contract_cols(grad_projected, qkv_weight).astype(jnp.bfloat16),...  35.7 us
    reduce_scatter x1, waiting for transfers between devices, shards(): lax.psum_scatter(down_part.astype(jnp.bfloat16), 'tensor', scatter_dimens...  31.7 us
    all_gather x1, waiting for transfers between devices, shards(): lax.all_gather(tokens, 'tensor', axis=1, tiled=True).astype(jnp.float32)  25.7 us
    dot_general x4, matrix products, contract_rows(): lax.dot_general(left, right, (((0,), (0,)), ((), ())), preferred_element_...  24.3 us
  transfers between devices with their start and end apart: 8, of which 8 were waited for; matrix products, arithmetic and copies ran while one was open for 5% of the time, Pallas kernels for 0%

commit v1 on v0

--- a/solution.py
+++ b/solution.py
@@ -52,6 +52,95 @@
         "iqhd,ikhd->ihqk", query_rows, key_rows, preferred_element_type=jnp.float32
     ) * HD ** (-0.5)
     return jnp.exp(scores - log_total[..., None])
+
+
+def exchange(block, axis, bit):
+    size = lax.axis_size(axis)
+    return lax.ppermute(block, axis, [(index, index ^ (1 << bit)) for index in range(size)])
+
+
+def bit_of(axis, bit):
+    return (lax.axis_index(axis) >> bit) % 2 == 1
+
+
+def bits_in(axis):
+    return (lax.axis_size(axis) - 1).bit_length()
+
+
+def gather_cols(block, axis):
+    width = block.shape[-1]
+    for bit in range(1, bits_in(axis)):
+        got = exchange(block, axis, bit)
+        upper = bit_of(axis, bit)
+        block = jnp.concatenate(
+            [jnp.where(upper, got, block), jnp.where(upper, block, got)], axis=-1
+        )
+    got = exchange(block, axis, 0)
+    upper = bit_of(axis, 0)
+    pieces = []
+    for start in range(0, block.shape[-1], width):
+        mine, theirs = (part[..., start : start + width] for part in (block, got))
+        pieces += [jnp.where(upper, theirs, mine), jnp.where(upper, mine, theirs)]
+    return jnp.concatenate(pieces, axis=-1)
+
+
+def sum_all(part, axis):
+    half = part.shape[-1] // 2
+    upper = bit_of(axis, 0)
+    low, high = part[..., :half], part[..., half:]
+    got = exchange(jnp.where(upper, low, high), axis, 0)
+    total = jnp.where(upper, high, low).astype(jnp.float32) + got.astype(jnp.float32)
+    for bit in range(1, bits_in(axis)):
+        sent = total.astype(jnp.bfloat16)
+        got = exchange(sent, axis, bit)
+        total = sent.astype(jnp.float32) + got.astype(jnp.float32)
+    sent = total.astype(jnp.bfloat16)
+    got = exchange(sent, axis, 0)
+    return jnp.concatenate([jnp.where(upper, got, sent), jnp.where(upper, sent, got)], axis=-1)
+
+
+def sum_scatter_cols(part, axis):
+    count = lax.axis_size(axis)
+    width = part.shape[-1] // count
+    upper = bit_of(axis, 0)
+    blocks = [part[..., index * width : (index + 1) * width] for index in range(count)]
+    even = jnp.concatenate(blocks[0::2], axis=-1)
+    odd = jnp.concatenate(blocks[1::2], axis=-1)
+    got = exchange(jnp.where(upper, even, odd), axis, 0)
+    total = jnp.where(upper, odd, even).astype(jnp.float32) + got.astype(jnp.float32)
+    for bit in reversed(range(1, bits_in(axis))):
+        half = total.shape[-1] // 2
+        upper = bit_of(axis, bit)
+        low, high = total[..., :half], total[..., half:]
+        got = exchange(jnp.where(upper, low, high).astype(jnp.bfloat16), axis, bit)
+        total = jnp.where(upper, high, low) + got.astype(jnp.float32)
+    return total
+
+
+def sum_rows(grad, axis, order):
+    for bit in order:
+        half = grad.shape[0] // 2
+        upper = bit_of(axis, bit)
+        low, high = grad[:half], grad[half:]
+        got = exchange(jnp.where(upper, low, high).astype(jnp.bfloat16), axis, bit)
+        grad = jnp.where(upper, high, low) + got.astype(jnp.float32)
+    grad = grad.astype(jnp.bfloat16)
+    for bit in reversed(order):
+        got = exchange(grad, axis, bit)
+        upper = bit_of(axis, bit)
+        grad = jnp.concatenate([jnp.where(upper, got, grad), jnp.where(upper, grad, got)], axis=0)
+    return grad.astype(jnp.float32)
+
+
+def sum_small(values, axis):
+    packed = jnp.concatenate(values)
+    for bit in range(bits_in(axis)):
+        packed = packed + exchange(packed, axis, bit)
+    result, start = [], 0
+    for value in values:
+        result.append(packed[start : start + value.shape[0]])
+        start += value.shape[0]
+    return result
 
 
 def shards(
@@ -73,7 +162,9 @@
     layer_scale2,
     cotangent,
 ):
-    whole = lax.all_gather(tokens, "tensor", axis=1, tiled=True).astype(jnp.float32)
+    whole = gather_cols(tokens, "tensor").astype(jnp.float32)
+    upstream = gather_cols(cotangent, "tensor").astype(jnp.float32)
+    scale2_all = lax.all_gather(layer_scale2, "tensor", axis=0, tiled=True)
     row_count = whole.shape[0]
     images = row_count // TOK_IMG
     heads_local = qkv_weight.shape[1] // (3 * HD)
@@ -110,9 +201,7 @@
         .reshape(row_count, heads_local * HD)
     )
     attention_part = jnp.dot(mixed, out_weight, preferred_element_type=jnp.float32)
-    attended = (
-        lax.psum(attention_part.astype(jnp.bfloat16), "tensor").astype(jnp.float32) + out_bias
-    )
+    attended = sum_all(attention_part.astype(jnp.bfloat16), "tensor").astype(jnp.float32) + out_bias
     residual = whole + layer_scale1 * attended
     normed2, inv_std2, scaled2 = layer_norm(residual, norm2_gain, norm2_bias)
     lowered2 = scaled2.astype(jnp.bfloat16)
@@ -120,12 +209,7 @@
     activated, slope = gelu_parts(hidden_pre)
     activated_low = activated.astype(jnp.bfloat16)
     down_part = jnp.dot(activated_low, down_weight, preferred_element_type=jnp.float32)
-    branch_cols = (
-        lax.psum_scatter(
-            down_part.astype(jnp.bfloat16), "tensor", scatter_dimension=1, tiled=True
-        ).astype(jnp.float32)
-        + down_bias
-    )
+    branch_cols = sum_scatter_cols(down_part.astype(jnp.bfloat16), "tensor") + down_bias
     width_local = tokens.shape[1]
     col_start = lax.axis_index("tensor") * width_local
     residual_cols = lax.dynamic_slice_in_dim(residual, col_start, width_local, 1)
@@ -133,19 +217,14 @@
     upstream_cols = cotangent.astype(jnp.float32)
     grad_layer_scale2 = jnp.sum(upstream_cols * branch_cols, axis=0)
     grad_down_bias = jnp.sum(upstream_cols * layer_scale2, axis=0)
-    branch_grad_cols = (upstream_cols * layer_scale2).astype(jnp.bfloat16)
-    branch_grad, upstream_low = (
-        lax.all_gather(branch_grad_cols, "tensor", axis=1, tiled=True),
-        lax.all_gather(cotangent, "tensor", axis=1, tiled=True),
-    )
-    upstream = upstream_low.astype(jnp.float32)
+    branch_grad = (upstream * scale2_all).astype(jnp.bfloat16)
     grad_down_weight = contract_rows(activated_low, branch_grad)
     grad_hidden = contract_cols(branch_grad, down_weight)
     grad_pre = grad_hidden * slope
     grad_up_bias = jnp.sum(grad_pre, axis=0)
     grad_pre_low = grad_pre.astype(jnp.bfloat16)
     grad_up_weight = contract_rows(lowered2, grad_pre_low)
-    grad_lowered2 = lax.psum(
+    grad_lowered2 = sum_all(
         contract_cols(grad_pre_low, up_weight).astype(jnp.bfloat16), "tensor"
     ).astype(jnp.float32)
     grad_norm2_gain = jnp.sum(grad_lowered2 * normed2, axis=0)
@@ -182,49 +261,65 @@
         .astype(jnp.bfloat16)
     )
     grad_qkv_weight = contract_rows(lowered1, grad_projected)
-    grad_lowered1 = lax.psum(
+    def cols(values):
+        return lax.dynamic_slice_in_dim(values, col_start, width_local, values.ndim - 1)
+
+    grad_lowered1 = sum_scatter_cols(
         contract_cols(grad_projected, qkv_weight).astype(jnp.bfloat16), "tensor"
-    ).astype(jnp.float32)
-    grad_norm1_gain = jnp.sum(grad_lowered1 * normed1, axis=0)
-    grad_norm1_bias = jnp.sum(grad_lowered1, axis=0)
-    grad_whole = grad_residual + norm_back(grad_lowered1, normed1, inv_std1, norm1_gain)
-    input_grad = lax.dynamic_slice_in_dim(grad_whole, col_start, width_local, 1)
+    )
+    normed1_cols = cols(normed1)
+    features = whole.shape[1]
+    scaled = grad_lowered1 * cols(norm1_gain)
+    row_sums = sum_small(
+        [jnp.sum(scaled, axis=-1), jnp.sum(scaled * normed1_cols, axis=-1)], "tensor"
+    )
+    mean_scaled, mean_product = (values[:, None] / features for values in row_sums)
+    input_grad = cols(grad_residual) + inv_std1 * (
+        scaled - mean_scaled - normed1_cols * mean_product
+    )
+    order = tuple(range(bits_in("dp")))
+    swapped = order[1:2] + order[:1] + order[2:]
+    grad_down_weight = sum_rows(grad_down_weight, "dp", order)
+    grad_up_weight = sum_rows(grad_up_weight, "dp", swapped)
+    grad_out_weight = sum_rows(grad_out_weight, "dp", order)
+    middle = grad_qkv_weight.shape[0] // 2
+    grad_qkv_weight = jnp.concatenate(
+        [
+            sum_rows(grad_qkv_weight[:middle], "dp", order),
+            sum_rows(grad_qkv_weight[middle:], "dp", swapped),
+        ],
+        axis=0,
+    )
     (
-        grad_norm1_gain,
-        grad_norm1_bias,
-        grad_qkv_weight,
         grad_query_bias,
         grad_value_bias,
-        grad_out_weight,
         grad_out_bias,
         grad_layer_scale1,
         grad_norm2_gain,
         grad_norm2_bias,
-        grad_up_weight,
         grad_up_bias,
-        grad_down_weight,
         grad_down_bias,
         grad_layer_scale2,
-    ) = lax.psum(
-        (
-            grad_norm1_gain,
-            grad_norm1_bias,
-            grad_qkv_weight,
+    ) = sum_small(
+        [
             grad_query_bias,
             grad_value_bias,
-            grad_out_weight,
             grad_out_bias,
             grad_layer_scale1,
             grad_norm2_gain,
             grad_norm2_bias,
-            grad_up_weight,
             grad_up_bias,
-            grad_down_weight,
             grad_down_bias,
             grad_layer_scale2,
-        ),
+        ],
         "dp",
     )
+    norm1_sums = jnp.stack(
+        sum_small(
+            [jnp.sum(grad_lowered1 * normed1_cols, axis=0), jnp.sum(grad_lowered1, axis=0)], "dp"
+        )
+    )
+    grad_norm1_gain, grad_norm1_bias = gather_cols(norm1_sums, "tensor")
     return (
         output,
         input_grad,

time: 816 us -> 401 us (0.49)
  waiting for transfers between devices: 590 us -> 169 us
  starting transfers between devices: 0.32 us -> 60.1 us
  blocking collectives: 39.7 us -> 5.25 us
  matrix products: 89.5 us -> 72.1 us
  other arithmetic: 36.2 us -> 51.9 us
  between operations: 14.7 us -> 2.45 us
    psum x4 -> x0, waiting for transfers between devices: 488 us -> none  [the longest x1 358 us: shards(): lax.psum((grad_norm1_gain, grad_norm1_bias, grad_qkv_weight, grad_query_b...]
    ppermute x0 -> x54, waiting for transfers between devices: none -> 169 us  [exchange(): lax.ppermute(block, axis, [(index, index ^ 1 << bit) for index in range(s...]
    all_gather x3 -> x0, waiting for transfers between devices: 68.7 us -> none  [the longest x1 25.7 us: shards(): lax.all_gather(tokens, 'tensor', axis=1, tiled=True).astype(jnp.float32)]
    ppermute x0 -> x54, starting transfers between devices: none -> 60.1 us  [exchange(): lax.ppermute(block, axis, [(index, index ^ 1 << bit) for index in range(s...]
    psum x1 -> x0, blocking collectives: 39.7 us -> none  [shards(): lax.psum((grad_norm1_gain, grad_norm1_bias, grad_qkv_weight, grad_query_b...]
    reduce_scatter x1 -> x0, waiting for transfers between devices: 31.7 us -> none  [shards(): lax.psum_scatter(down_part.astype(jnp.bfloat16), 'tensor', scatter_dimens...]
    select_n x0 -> x27, other arithmetic: none -> 12.2 us  [the longest x15 4.76 us: sum_rows(): jnp.where(upper, got, grad)]
    unnamed x66 -> x116, local copies, waits for them, and re-layouts: 16.8 us -> 5.87 us
  transfers between devices with their start and end apart: 8 -> 54, of which waited for: 8 -> 31; matrix products, arithmetic and copies ran while one was open for 5% -> 24% of each run, Pallas kernels for 0% -> 0%
where the time goes in v1:
time: 401 us; the launch traced here: 396 us
  waiting for transfers between devices  169 us (42%)
  matrix products  72.1 us (18%)
  starting transfers between devices  60.1 us (15%)
  other arithmetic  51.9 us (13%)
  local copies, waits for them, and re-layouts  35.5 us (9%)
  blocking collectives  5.25 us (1%)
    ppermute x54, waiting for transfers between devices, exchange(): lax.ppermute(block, axis, [(index, index ^ 1 << bit) for index in range(s...  169 us
    ppermute x54, starting transfers between devices, exchange(): lax.ppermute(block, axis, [(index, index ^ 1 << bit) for index in range(s...  60.1 us
    dot_general x4, matrix products, contract_rows(): lax.dot_general(left, right, (((0,), (0,)), ((), ())), preferred_element_...  15.2 us
    dot_general x1, matrix products, shards(): jnp.einsum('ihqk,iqhd->ikhd', grad_scores, query_rows, preferred_element_...  12.8 us
    dot_general x1, matrix products, shards(): jnp.einsum('ihqk,ikhd->iqhd', grad_scores, key_rows, preferred_element_ty...  11.3 us
    dot_general x4, matrix products, contract_cols(): lax.dot_general(left, right, (((1,), (1,)), ((), ())), preferred_element_...  10.6 us
  transfers between devices with their start and end apart: 54, of which 31 were waited for; matrix products, arithmetic and copies ran while one was open for 24% of the time, Pallas kernels for 0%

profile of v1, /device:TPU:0, one launch (start us, length us, event | category | flops | bytes accessed | tf_op | source)
XLA Modules:
  0.0 396.4 jit_solution(13702693248344332426)
XLA Ops:
  3.7 12.2 %collective-permute-done = bf16[1028,256]{1,0:T(8,128)(2,1)S(1)} collective-permute-done((bf16[1028,256]{1,0:T(8,128)(2,1)}, bf16[1028,256]{1,0:T(8,128)(2,1)S(1)}, u32[]{:S(2)}, u32[]{:S(2)}) %collective-permute-start) | collective-permute-done | bytes 526368 | tf_op jit(solution)/shard_map/ppermute | solution.py:59
  32.5 3.1 squeeze.8
  35.7 3.1 squeeze.7
  57.5 10.8 %collective-permute-done.7 = bf16[1028,256]{1,0:T(8,128)(2,1)S(1)} collective-permute-done((bf16[1028,256]{1,0:T(8,128)(2,1)S(1)}, bf16[1028,256]{1,0:T(8,128)(2,1)S(1)}, u32[]{:S(2)}, u32[]{:S(2)}) %collective-permute-start.7) | collective-permute-done | bytes 526368 | tf_op jit(solution)/shard_map/ppermute | solution.py:59
  70.3 19.8 %collective-permute-done.3 = bf16[1028,512]{1,0:T(8,128)(2,1)S(1)} collective-permute-done((bf16[1028,512]{1,0:T(8,128)(2,1)S(1)}, bf16[1028,512]{1,0:T(8,128)(2,1)S(1)}, u32[]{:S(2)}, u32[]{:S(2)}) %collective-permute-start.3) | collective-permute-done | bytes 1052704 | tf_op jit(solution)/shard_map/ppermute | solution.py:59
  91.5 5.3 %all-gather = f32[4,1,256]{2,1,0:T(1,128)S(1)} all-gather(f32[1,1,256]{2,1,0:T(1,128)S(1)} %bitcast.69), channel_id=1, replica_groups=mesh['dp'=8,'tensor'=4] {'tensor'}, dimensions={0}, use_global_device_ids=true | all-gather | bytes 5120 | tf_op jit(solution)/shard_map/all_gather | solution.py:167
  100.3 5.1 %fusion.76 = (f32[1028]{0:T(1024)S(1)}, f32[1028,1024]{1,0:T(8,128)S(1)}, f32[1028,1024]{1,0:T(8,128)}) fusion(f32[1024]{0:T(1024)S(1)} %copy-done.39, bf16[1028,512]{1,0:T(8,128)(2,1)S(1)} %get-tuple-element.52, bf16[1028,512]{1,0:T(8,128)(2,1)S(1)} %get-tuple-element.51, f32[1024]{0:T(1024)S(1)} %copy-done.38, bf16[1028,256]{1,0:T(8,128)(2,1)S(1)} %copy-done.5, ...), kind=kLoop, calls=%fused_computation.245 | loop fusion | flops 18947068 | bytes 12652592 | tf_op jit(solution)/shard_map/reduce_sum | solution.py:16
  109.2 4.0 %fusion.86 = (f32[1024]{0:T(1024)S(1)}, bf16[1028,1024]{1,0:T(8,128)(2,1)S(1)}) fusion(f32[1028,1024]{1,0:T(8,128)S(1)} %get-tuple-element.125, bf16[1024,1024]{1,0:T(8,128)(2,1)S(1)} %copy-done.46, f32[1024]{0:T(1024)S(1)} %bitcast.70, bf16[1028,256]{1,0:T(8,128)(2,1)S(1)} %get-tuple-element.65, bf16[1028,256]{1,0:T(8,128)(2,1)S(1)} %get-tuple-element.66, ...), kind=kOutput, calls=%fused_computation.253 | convolution fusion | flops 2177977344 | bytes 10526720 | tf_op jit(solution)/shard_map/dot_general | solution.py:45
  115.7 3.5 fusion.46
  129.2 21.3 %collective-permute-done.42 = bf16[512,1024]{1,0:T(8,128)(2,1)S(1)} collective-permute-done((bf16[512,1024]{1,0:T(8,128)(2,1)S(1)}, bf16[512,1024]{1,0:T(8,128)(2,1)S(1)}, u32[]{:S(2)}, u32[]{:S(2)}) %collective-permute-start.42) | collective-permute-done | bytes 1048608 | tf_op jit(solution)/shard_map/ppermute | solution.py:59
  157.9 6.6 %collective-permute-done.43 = bf16[256,1024]{1,0:T(8,128)(2,1)S(1)} collective-permute-done((bf16[256,1024]{1,0:T(8,128)(2,1)S(1)}, bf16[256,1024]{1,0:T(8,128)(2,1)S(1)}, u32[]{:S(2)}, u32[]{:S(2)}) %collective-permute-start.43) | collective-permute-done | bytes 524320 | tf_op jit(solution)/shard_map/ppermute | solution.py:59
  170.6 15.0 %collective-permute-done.44 = bf16[128,1024]{1,0:T(8,128)(2,1)S(1)} collective-permute-done((bf16[128,1024]{1,0:T(8,128)(2,1)S(1)}, bf16[128,1024]{1,0:T(8,128)(2,1)S(1)}, u32[]{:S(2)}, u32[]{:S(2)}) %collective-permute-start.44) | collective-permute-done | bytes 262176 | tf_op jit(solution)/shard_map/ppermute | solution.py:59
  187.4 9.4 %collective-permute-done.50 = bf16[128,1024]{1,0:T(8,128)(2,1)S(1)} collective-permute-done((bf16[128,1024]{1,0:T(8,128)(2,1)S(1)}, bf16[128,1024]{1,0:T(8,128)(2,1)S(1)}, u32[]{:S(2)}, u32[]{:S(2)}) %collective-permute-start.50) | collective-permute-done | bytes 262176 | tf_op jit(solution)/shard_map/ppermute | solution.py:59
  197.0 11.1 %collective-permute-done.45 = bf16[128,1024]{1,0:T(8,128)(2,1)S(1)} collective-permute-done((bf16[128,1024]{1,0:T(8,128)(2,1)S(1)}, bf16[128,1024]{1,0:T(8,128)(2,1)S(1)}, u32[]{:S(2)}, u32[]{:S(2)}) %collective-permute-start.45) | collective-permute-done | bytes 262176 | tf_op jit(solution)/shard_map/ppermute | solution.py:59
  208.2 3.6 collective-permute-done.51
  218.7 3.5 collective-permute-start.47
  222.2 4.6 %collective-permute-done.52 = bf16[256,1024]{1,0:T(8,128)(2,1)S(1)} collective-permute-done((bf16[256,1024]{1,0:T(8,128)(2,1)S(1)}, bf16[256,1024]{1,0:T(8,128)(2,1)S(1)}, u32[]{:S(2)}, u32[]{:S(2)}) %collective-permute-start.52) | collective-permute-done | bytes 524320 | tf_op jit(solution)/shard_map/ppermute | solution.py:59
  231.9 3.3 multiply_reduce_fusion.2
  239.9 5.2 %bitcast_reduce_fusion = (f32[4,64]{1,0:T(4,128)S(1)}, bf16[4,4,64,257]{3,2,1,0:T(8,128)(2,1)}) fusion(bf16[4,257,4,64]{1,3,2,0:T(8,128)(2,1)S(1)} %copy.63, f32[4,4,257,257]{2,3,1,0:T(8,128)} %copy-done.2, f32[4,4,257]{2,1,0:T(4,128)S(1)} %log_add_fusion), kind=kOutput, calls=%fused_computation.74 | convolution fusion | flops 138964784 | bytes 5297280 | tf_op jit(solution)/shard_map/ihqk,iqhd->ikhd/dot_general | solution.py:239
  245.1 4.1 %fusion.52 = f32[4,4,257,257]{2,3,1,0:T(8,128)} fusion(bf16[4,257,4,64]{1,3,2,0:T(8,128)(2,1)S(1)} %copy.63, bf16[4,257,4,64]{1,0,3,2:T(4,128)(2,1)S(1)} %copy-done.13), kind=kOutput, calls=%fused_computation.132 | convolution fusion | flops 135268352 | bytes 5279808 | tf_op jit(solution)/shard_map/iqhd,ikhd->ihqk/dot_general | solution.py:245
  249.2 12.8 %fusion.40 = bf16[4,257,4,1,64]{1,4,2,0,3:T(8,128)(2,1)} fusion(f32[4,4,257,257]{2,3,1,0:T(8,128)} %fusion.52, f32[4,4,257,257]{2,3,1,0:T(8,128)} %copy-done.2, f32[4,4,257]{2,1,0:T(4,128)S(1)} %log_add_fusion, bf16[4,257,4,64]{1,0,3,2:T(4,128)(2,1)} %copy-done.18), kind=kOutput, calls=%fused_computation.84 | convolution fusion | flops 145046944 | bytes 9523392 | tf_op jit(solution)/shard_map/ihqk,iqhd->ikhd/dot_general | solution.py:253
  262.0 11.3 %bitcast_reduce_fusion.1 = (f32[4,64]{1,0:T(4,128)S(1)}, bf16[4,4,64,257]{3,2,1,0:T(8,128)(2,1)}) fusion(f32[4,4,257,257]{2,3,1,0:T(8,128)} %fusion.52, f32[4,4,257,257]{2,3,1,0:T(8,128)} %copy-done.2, f32[4,4,257]{2,1,0:T(4,128)S(1)} %log_add_fusion, bf16[4,257,4,64]{1,0,3,2:T(4,128)(2,1)S(1)} %copy-done.17), kind=kOutput, calls=%fused_computation.76 | convolution fusion | flops 145309856 | bytes 9524416 | tf_op jit(solution)/shard_map/ihqk,ikhd->iqhd/dot_general | solution.py:250
  275.2 3.2 copy.71
  278.4 5.0 %convert_element_type.291 = bf16[1028,768]{0,1:T(8,128)(2,1)} reshape(bf16[4,257,4,3,64]{1,0,4,3,2:T(4,128)(2,1)} %copy.71) | data formatting | bytes 3158016 | tf_op jit(solution)/shard_map/convert_element_type | solution.py:261
  283.5 6.3 %fusion.60 = f32[1024,768]{1,0:T(8,128)} fusion(bf16[1028,768]{0,1:T(8,128)(2,1)} %convert_element_type.291, f32[1024]{0:T(1024)S(1)} %copy-done.51, f32[1024]{0:T(1024)S(1)} %copy-done.45, f32[1028]{0:T(1024)S(1)} %add_rsqrt_fusion.1, f32[1028]{0:T(1024)S(1)} %broadcast_multiply_fusion.3, bf16[1028,256]{1,0:T(8,128)(2,1)S(1)} %copy-done.6, ...), kind=kOutput, calls=%fused_computation.140 | convolution fusion | flops 1630588928 | bytes 6846496 | tf_op jit(solution)/shard_map/dot_general | solution.py:39
  289.8 3.4 convolution_convert_fusion
  312.1 5.9 %collective-permute-done.37 = bf16[64,1024]{1,0:T(8,128)(2,1)S(1)} collective-permute-done((bf16[64,1024]{1,0:T(8,128)(2,1)S(1)}, bf16[64,1024]{1,0:T(8,128)(2,1)S(1)}, u32[]{:S(2)}, u32[]{:S(2)}) %collective-permute-start.37) | collective-permute-done | bytes 131104 | tf_op jit(solution)/shard_map/ppermute | solution.py:59
  321.8 3.2 collective-permute-done.38
  325.5 3.4 collective-permute-start.39
  344.4 5.0 %collective-permute-done.29 = bf16[64,768]{1,0:T(8,128)(2,1)S(1)} collective-permute-done((bf16[64,768]{1,0:T(8,128)(2,1)S(1)}, bf16[64,768]{1,0:T(8,128)(2,1)S(1)}, u32[]{:S(2)}, u32[]{:S(2)}) %collective-permute-start.29) | collective-permute-done | bytes 98336 | tf_op jit(solution)/shard_map/ppermute | solution.py:59
  352.5 4.7 %collective-permute-done.30 = bf16[64,768]{1,0:T(8,128)(2,1)S(1)} collective-permute-done((bf16[64,768]{1,0:T(8,128)(2,1)S(1)}, bf16[64,768]{1,0:T(8,128)(2,1)S(1)}, u32[]{:S(2)}, u32[]{:S(2)}) %collective-permute-start.30) | collective-permute-done | bytes 98336 | tf_op jit(solution)/shard_map/ppermute | solution.py:59
  366.8 6.2 %collective-permute-done.13 = bf16[1028,256]{1,0:T(8,128)(2,1)S(1)} collective-permute-done((bf16[1028,256]{1,0:T(8,128)(2,1)S(1)}, bf16[1028,256]{1,0:T(8,128)(2,1)S(1)}, u32[]{:S(2)}, u32[]{:S(2)}) %collective-permute-start.13) | collective-permute-done | bytes 526368 | tf_op jit(solution)/shard_map/ppermute | solution.py:59
  (351 shorter events, 168.9 us)
Async XLA Ops:
  0.7 15.2 %collective-permute-start = (bf16[1028,256]{1,0:T(8,128)(2,1)}, bf16[1028,256]{1,0:T(8,128)(2,1)S(1)}, u32[]{:S(2)}, u32[]{:S(2)}) collective-permute-start(bf16[1028,256]{1,0:T(8,128)(2,1)} %param.17), channel_id=1, source_target_pairs={{0,2},{1,3},{2,0},{3,1},{4,6},{5,7},{6,4},{7,5},{8,10},{9,11},{10,... | collective-permute-start | bytes 1579016 | tf_op jit(solution)/shard_map/ppermute | solution.py:59
  53.5 14.9 %collective-permute-start.7 = (bf16[1028,256]{1,0:T(8,128)(2,1)S(1)}, bf16[1028,256]{1,0:T(8,128)(2,1)S(1)}, u32[]{:S(2)}, u32[]{:S(2)}) collective-permute-start(bf16[1028,256]{1,0:T(8,128)(2,1)S(1)} %copy-done.32), channel_id=1, source_target_pairs={{0,2},{1,3},{2,0},{3,1},{4,6},{5,7},{6,4},{7,5},{8,10},{9,11},{10,... | collective-permute-start | bytes 1579016 | tf_op jit(solution)/shard_map/ppermute | solution.py:59
  55.7 34.4 %collective-permute-start.3 = (bf16[1028,512]{1,0:T(8,128)(2,1)S(1)}, bf16[1028,512]{1,0:T(8,128)(2,1)S(1)}, u32[]{:S(2)}, u32[]{:S(2)}) collective-permute-start(bf16[1028,512]{1,0:T(8,128)(2,1)S(1)} %add_convert_fusion.5), channel_id=1, source_target_pairs={{0,2},{1,3},{2,0},{3,1},{4,6},{5,7},{6,4},{7,5},{8,10},{9,11},{10,... | collective-permute-start | bytes 3158024 | tf_op jit(solution)/shard_map/ppermute | solution.py:59
  70.3 26.5 %collective-permute-start.8 = (bf16[1028,512]{1,0:T(8,128)(2,1)}, bf16[1028,512]{1,0:T(8,128)(2,1)}, u32[]{:S(2)}, u32[]{:S(2)}) collective-permute-start(bf16[1028,512]{1,0:T(8,128)(2,1)} %pad_maximum_fusion.8), channel_id=1, source_target_pairs={{0,1},{1,0},{2,3},{3,2},{4,5},{5,4},{6,7},{7,6},{8,9},{9,8},{10,11... | collective-permute-start | bytes 3158024 | tf_op jit(solution)/shard_map/ppermute | solution.py:59
  124.7 30.8 %collective-permute-start.9 = (bf16[1028,512]{1,0:T(8,128)(2,1)S(1)}, bf16[1028,512]{1,0:T(8,128)(2,1)S(1)}, u32[]{:S(2)}, u32[]{:S(2)}) collective-permute-start(bf16[1028,512]{1,0:T(8,128)(2,1)S(1)} %broadcast_select_fusion.3), channel_id=1, source_target_pairs={{0,1},{1,0},{2,3},{3,2},{4,5},{5,4},{6,7},{7,6},{8,9},{9,8},{10,11... | collective-permute-start | bytes 3158024 | tf_op jit(solution)/shard_map/ppermute | solution.py:59
  125.3 25.3 %collective-permute-start.42 = (bf16[512,1024]{1,0:T(8,128)(2,1)S(1)}, bf16[512,1024]{1,0:T(8,128)(2,1)S(1)}, u32[]{:S(2)}, u32[]{:S(2)}) collective-permute-start(bf16[512,1024]{1,0:T(8,128)(2,1)S(1)} %select_convert_fusion.1), channel_id=1, source_target_pairs={{0,8},{4,12},{8,0},{12,4},{16,24},{20,28},{24,16},{28,20},{1,9},{5... | collective-permute-start | bytes 3145736 | tf_op jit(solution)/shard_map/ppermute | solution.py:59
  127.1 25.7 %collective-permute-start.48 = (bf16[512,1024]{1,0:T(8,128)(2,1)S(1)}, bf16[512,1024]{1,0:T(8,128)(2,1)S(1)}, u32[]{:S(2)}, u32[]{:S(2)}) collective-permute-start(bf16[512,1024]{1,0:T(8,128)(2,1)S(1)} %select_convert_fusion), channel_id=1, source_target_pairs={{0,4},{4,0},{8,12},{12,8},{16,20},{20,16},{24,28},{28,24},{1,5},{5... | collective-permute-start | bytes 3145736 | tf_op jit(solution)/shard_map/ppermute | solution.py:59
  129.2 28.3 %collective-permute-start.5 = (bf16[1028,512]{1,0:T(8,128)(2,1)S(1)}, bf16[1028,512]{1,0:T(8,128)(2,1)S(1)}, u32[]{:S(2)}, u32[]{:S(2)}) collective-permute-start(bf16[1028,512]{1,0:T(8,128)(2,1)S(1)} %broadcast_select_fusion.4), channel_id=1, source_target_pairs={{0,1},{1,0},{2,3},{3,2},{4,5},{5,4},{6,7},{7,6},{8,9},{9,8},{10,11... | collective-permute-start | bytes 3158024 | tf_op jit(solution)/shard_map/ppermute | solution.py:59
  151.3 13.3 %collective-permute-start.43 = (bf16[256,1024]{1,0:T(8,128)(2,1)S(1)}, bf16[256,1024]{1,0:T(8,128)(2,1)S(1)}, u32[]{:S(2)}, u32[]{:S(2)}) collective-permute-start(bf16[256,1024]{1,0:T(8,128)(2,1)S(1)} %select_convert_fusion.5), channel_id=1, source_target_pairs={{0,4},{4,0},{8,12},{12,8},{16,20},{20,16},{24,28},{28,24},{1,5},{5... | collective-permute-start | bytes 1572872 | tf_op jit(solution)/shard_map/ppermute | solution.py:59
  153.8 13.7 %collective-permute-start.49 = (bf16[256,1024]{1,0:T(8,128)(2,1)S(1)}, bf16[256,1024]{1,0:T(8,128)(2,1)S(1)}, u32[]{:S(2)}, u32[]{:S(2)}) collective-permute-start(bf16[256,1024]{1,0:T(8,128)(2,1)S(1)} %select_convert_fusion.4), channel_id=1, source_target_pairs={{0,8},{4,12},{8,0},{12,4},{16,24},{20,28},{24,16},{28,20},{1,9},{5... | collective-permute-start | bytes 1572872 | tf_op jit(solution)/shard_map/ppermute | solution.py:59
  155.9 56.7 %collective-permute-start.10 = (bf16[1028,512]{1,0:T(8,128)(2,1)S(1)}, bf16[1028,512]{1,0:T(8,128)(2,1)S(1)}, u32[]{:S(2)}, u32[]{:S(2)}) collective-permute-start(bf16[1028,512]{1,0:T(8,128)(2,1)S(1)} %add_convert_fusion.3), channel_id=1, source_target_pairs={{0,2},{1,3},{2,0},{3,1},{4,6},{5,7},{6,4},{7,5},{8,10},{9,11},{10,... | collective-permute-start | bytes 3158024 | tf_op jit(solution)/shard_map/ppermute | solution.py:59
  164.8 20.7 %collective-permute-start.44 = (bf16[128,1024]{1,0:T(8,128)(2,1)S(1)}, bf16[128,1024]{1,0:T(8,128)(2,1)S(1)}, u32[]{:S(2)}, u32[]{:S(2)}) collective-permute-start(bf16[128,1024]{1,0:T(8,128)(2,1)S(1)} %select_convert_fusion.9), channel_id=1, source_target_pairs={{0,16},{4,20},{8,24},{12,28},{16,0},{20,4},{24,8},{28,12},{1,17},{... | collective-permute-start | bytes 786440 | tf_op jit(solution)/shard_map/ppermute | solution.py:59
  167.8 29.0 %collective-permute-start.50 = (bf16[128,1024]{1,0:T(8,128)(2,1)S(1)}, bf16[128,1024]{1,0:T(8,128)(2,1)S(1)}, u32[]{:S(2)}, u32[]{:S(2)}) collective-permute-start(bf16[128,1024]{1,0:T(8,128)(2,1)S(1)} %select_convert_fusion.8), channel_id=1, source_target_pairs={{0,16},{4,20},{8,24},{12,28},{16,0},{20,4},{24,8},{28,12},{1,17},{... | collective-permute-start | bytes 786440 | tf_op jit(solution)/shard_map/ppermute | solution.py:59
  185.7 22.4 %collective-permute-start.45 = (bf16[128,1024]{1,0:T(8,128)(2,1)S(1)}, bf16[128,1024]{1,0:T(8,128)(2,1)S(1)}, u32[]{:S(2)}, u32[]{:S(2)}) collective-permute-start(bf16[128,1024]{1,0:T(8,128)(2,1)S(1)} %add_convert_fusion.11), channel_id=1, source_target_pairs={{0,16},{4,20},{8,24},{12,28},{16,0},{20,4},{24,8},{28,12},{1,17},{... | collective-permute-start | bytes 786440 | tf_op jit(solution)/shard_map/ppermute | solution.py:59
  185.8 27.2 %collective-permute-start.6 = (bf16[1028,256]{1,0:T(8,128)(2,1)S(1)}, bf16[1028,256]{1,0:T(8,128)(2,1)S(1)}, u32[]{:S(2)}, u32[]{:S(2)}) collective-permute-start(bf16[1028,256]{1,0:T(8,128)(2,1)S(1)} %select_convert_fusion.3), channel_id=1, source_target_pairs={{0,2},{1,3},{2,0},{3,1},{4,6},{5,7},{6,4},{7,5},{8,10},{9,11},{10,... | collective-permute-start | bytes 1579016 | tf_op jit(solution)/shard_map/ppermute | solution.py:59
  196.9 14.9 %collective-permute-start.51 = (bf16[128,1024]{1,0:T(8,128)(2,1)S(1)}, bf16[128,1024]{1,0:T(8,128)(2,1)S(1)}, u32[]{:S(2)}, u32[]{:S(2)}) collective-permute-start(bf16[128,1024]{1,0:T(8,128)(2,1)S(1)} %add_convert_fusion.10), channel_id=1, source_target_pairs={{0,16},{4,20},{8,24},{12,28},{16,0},{20,4},{24,8},{28,12},{1,17},{... | collective-permute-start | bytes 786440 | tf_op jit(solution)/shard_map/ppermute | solution.py:59
  211.9 14.9 %collective-permute-start.52 = (bf16[256,1024]{1,0:T(8,128)(2,1)S(1)}, bf16[256,1024]{1,0:T(8,128)(2,1)S(1)}, u32[]{:S(2)}, u32[]{:S(2)}) collective-permute-start(bf16[256,1024]{1,0:T(8,128)(2,1)S(1)} %pad_maximum_fusion.14), channel_id=1, source_target_pairs={{0,8},{4,12},{8,0},{12,4},{16,24},{20,28},{24,16},{28,20},{1,9},{5... | collective-permute-start | bytes 1572872 | tf_op jit(solution)/shard_map/ppermute | solution.py:59
  212.9 16.8 %collective-permute-start.11 = (bf16[1028,512]{1,0:T(8,128)(2,1)S(1)}, bf16[1028,512]{1,0:T(8,128)(2,1)S(1)}, u32[]{:S(2)}, u32[]{:S(2)}) collective-permute-start(bf16[1028,512]{1,0:T(8,128)(2,1)S(1)} %add_convert_fusion.2), channel_id=1, source_target_pairs={{0,1},{1,0},{2,3},{3,2},{4,5},{5,4},{6,7},{7,6},{8,9},{9,8},{10,11... | collective-permute-start | bytes 3158024 | tf_op jit(solution)/shard_map/ppermute | solution.py:59
  218.7 114.4 %collective-permute-start.47 = (bf16[512,1024]{1,0:T(8,128)(2,1)}, bf16[512,1024]{1,0:T(8,128)(2,1)}, u32[]{:S(2)}, u32[]{:S(2)}) collective-permute-start(bf16[512,1024]{1,0:T(8,128)(2,1)} %pad_maximum_fusion.11), channel_id=1, source_target_pairs={{0,8},{4,12},{8,0},{12,4},{16,24},{20,28},{24,16},{28,20},{1,9},{5... | collective-permute-start | bytes 3145736 | tf_op jit(solution)/shard_map/ppermute | solution.py:59
  228.2 97.3 %collective-permute-start.53 = (bf16[512,1024]{1,0:T(8,128)(2,1)}, bf16[512,1024]{1,0:T(8,128)(2,1)}, u32[]{:S(2)}, u32[]{:S(2)}) collective-permute-start(bf16[512,1024]{1,0:T(8,128)(2,1)} %pad_maximum_fusion.12), channel_id=1, source_target_pairs={{0,4},{4,0},{8,12},{12,8},{16,20},{20,16},{24,28},{28,24},{1,5},{5... | collective-permute-start | bytes 3145736 | tf_op jit(solution)/shard_map/ppermute | solution.py:59
  293.3 17.2 %collective-permute-start.36 = (bf16[128,1024]{1,0:T(8,128)(2,1)S(1)}, bf16[128,1024]{1,0:T(8,128)(2,1)S(1)}, u32[]{:S(2)}, u32[]{:S(2)}) collective-permute-start(bf16[128,1024]{1,0:T(8,128)(2,1)S(1)} %select_convert_fusion.10), channel_id=1, source_target_pairs={{0,4},{4,0},{8,12},{12,8},{16,20},{20,16},{24,28},{28,24},{1,5},{5... | collective-permute-start | bytes 786440 | tf_op jit(solution)/shard_map/ppermute | solution.py:59
  301.1 17.0 %collective-permute-start.21 = (bf16[256,768]{1,0:T(8,128)(2,1)S(1)}, bf16[256,768]{1,0:T(8,128)(2,1)S(1)}, u32[]{:S(2)}, u32[]{:S(2)}) collective-permute-start(bf16[256,768]{1,0:T(8,128)(2,1)S(1)} %get-tuple-element.37), channel_id=1, source_target_pairs={{0,4},{4,0},{8,12},{12,8},{16,20},{20,16},{24,28},{28,24},{1,5},{5... | collective-permute-start | bytes 1179656 | tf_op jit(solution)/shard_map/ppermute | solution.py:59
  308.7 12.2 %collective-permute-start.27 = (bf16[256,768]{1,0:T(8,128)(2,1)S(1)}, bf16[256,768]{1,0:T(8,128)(2,1)S(1)}, u32[]{:S(2)}, u32[]{:S(2)}) collective-permute-start(bf16[256,768]{1,0:T(8,128)(2,1)S(1)} %get-tuple-element.38), channel_id=1, source_target_pairs={{0,8},{4,12},{8,0},{12,4},{16,24},{20,28},{24,16},{28,20},{1,9},{5... | collective-permute-start | bytes 1179656 | tf_op jit(solution)/shard_map/ppermute | solution.py:59
  318.0 41.6 %collective-permute-start.12 = (bf16[1028,512]{1,0:T(8,128)(2,1)S(1)}, bf16[1028,512]{1,0:T(8,128)(2,1)S(1)}, u32[]{:S(2)}, u32[]{:S(2)}) collective-permute-start(bf16[1028,512]{1,0:T(8,128)(2,1)S(1)} %broadcast_select_fusion), channel_id=1, source_target_pairs={{0,1},{1,0},{2,3},{3,2},{4,5},{5,4},{6,7},{7,6},{8,9},{9,8},{10,11... | collective-permute-start | bytes 3158024 | tf_op jit(solution)/shard_map/ppermute | solution.py:59
  321.2 16.4 %collective-permute-start.28 = (bf16[128,768]{1,0:T(8,128)(2,1)S(1)}, bf16[128,768]{1,0:T(8,128)(2,1)S(1)}, u32[]{:S(2)}, u32[]{:S(2)}) collective-permute-start(bf16[128,768]{1,0:T(8,128)(2,1)S(1)} %select_convert_fusion.11), channel_id=1, source_target_pairs={{0,4},{4,0},{8,12},{12,8},{16,20},{20,16},{24,28},{28,24},{1,5},{5... | collective-permute-start | bytes 589832 | tf_op jit(solution)/shard_map/ppermute | solution.py:59
  325.0 13.8 %collective-permute-start.22 = (bf16[128,768]{1,0:T(8,128)(2,1)S(1)}, bf16[128,768]{1,0:T(8,128)(2,1)S(1)}, u32[]{:S(2)}, u32[]{:S(2)}) collective-permute-start(bf16[128,768]{1,0:T(8,128)(2,1)S(1)} %select_convert_fusion.12), channel_id=1, source_target_pairs={{0,8},{4,12},{8,0},{12,4},{16,24},{20,28},{24,16},{28,20},{1,9},{5... | collective-permute-start | bytes 589832 | tf_op jit(solution)/shard_map/ppermute | solution.py:59
  325.5 12.0 %collective-permute-start.39 = (bf16[32,1024]{1,0:T(8,128)(2,1)S(1)}, bf16[32,1024]{1,0:T(8,128)(2,1)S(1)}, u32[]{:S(2)}, u32[]{:S(2)}) collective-permute-start(bf16[32,1024]{1,0:T(8,128)(2,1)S(1)} %add_convert_fusion.14), channel_id=1, source_target_pairs={{0,16},{4,20},{8,24},{12,28},{16,0},{20,4},{24,8},{28,12},{1,17},{... | collective-permute-start | bytes 196616 | tf_op jit(solution)/shard_map/ppermute | solution.py:59
  337.7 11.7 %collective-permute-start.29 = (bf16[64,768]{1,0:T(8,128)(2,1)S(1)}, bf16[64,768]{1,0:T(8,128)(2,1)S(1)}, u32[]{:S(2)}, u32[]{:S(2)}) collective-permute-start(bf16[64,768]{1,0:T(8,128)(2,1)S(1)} %select_convert_fusion.14), channel_id=1, source_target_pairs={{0,16},{4,20},{8,24},{12,28},{16,0},{20,4},{24,8},{28,12},{1,17},{... | collective-permute-start | bytes 294920 | tf_op jit(solution)/shard_map/ppermute | solution.py:59
  338.9 12.2 %collective-permute-start.23 = (bf16[64,768]{1,0:T(8,128)(2,1)S(1)}, bf16[64,768]{1,0:T(8,128)(2,1)S(1)}, u32[]{:S(2)}, u32[]{:S(2)}) collective-permute-start(bf16[64,768]{1,0:T(8,128)(2,1)S(1)} %select_convert_fusion.15), channel_id=1, source_target_pairs={{0,16},{4,20},{8,24},{12,28},{16,0},{20,4},{24,8},{28,12},{1,17},{... | collective-permute-start | bytes 294920 | tf_op jit(solution)/shard_map/ppermute | solution.py:59
  343.8 14.5 %collective-permute-start.41 = (bf16[128,1024]{1,0:T(8,128)(2,1)S(1)}, bf16[128,1024]{1,0:T(8,128)(2,1)S(1)}, u32[]{:S(2)}, u32[]{:S(2)}) collective-permute-start(bf16[128,1024]{1,0:T(8,128)(2,1)S(1)} %pad_maximum_fusion.17), channel_id=1, source_target_pairs={{0,4},{4,0},{8,12},{12,8},{16,20},{20,16},{24,28},{28,24},{1,5},{5... | collective-permute-start | bytes 786440 | tf_op jit(solution)/shard_map/ppermute | solution.py:59
  360.1 12.9 %collective-permute-start.13 = (bf16[1028,256]{1,0:T(8,128)(2,1)S(1)}, bf16[1028,256]{1,0:T(8,128)(2,1)S(1)}, u32[]{:S(2)}, u32[]{:S(2)}) collective-permute-start(bf16[1028,256]{1,0:T(8,128)(2,1)S(1)} %select_convert_fusion.2), channel_id=1, source_target_pairs={{0,2},{1,3},{2,0},{3,1},{4,6},{5,7},{6,4},{7,5},{8,10},{9,11},{10,... | collective-permute-start | bytes 1579016 | tf_op jit(solution)/shard_map/ppermute | solution.py:59
  365.2 13.9 %collective-permute-start.26 = (bf16[256,768]{1,0:T(8,128)(2,1)S(1)}, bf16[256,768]{1,0:T(8,128)(2,1)S(1)}, u32[]{:S(2)}, u32[]{:S(2)}) collective-permute-start(bf16[256,768]{1,0:T(8,128)(2,1)S(1)} %pad_maximum_fusion.15), channel_id=1, source_target_pairs={{0,4},{4,0},{8,12},{12,8},{16,20},{20,16},{24,28},{28,24},{1,5},{5... | collective-permute-start | bytes 1179656 | tf_op jit(solution)/shard_map/ppermute | solution.py:59
  (76 other events, 468.8 us)

commit v2 on v0

v2 whole, which is shorter than its diff:
```python
import math

import jax
import jax.numpy as jnp
from jax import lax
from jax.experimental import pallas as pl
from jax.experimental.pallas import tpu as pltpu
from jax.sharding import PartitionSpec as P

HD = 64
TOK_IMG = 257


EPS = 1e-06


def layer_norm(values, gain, bias):
    row_mean = jnp.mean(values, axis=-1, keepdims=True)
    centred = values - row_mean
    inv_std = lax.rsqrt(jnp.mean(centred * centred, axis=-1, keepdims=True) + EPS)
    normed = centred * inv_std
    return (normed, inv_std, normed * gain + bias)


def norm_back(upstream, normed, inv_std, gain):
    scaled = upstream * gain
    return inv_std * (
        scaled
        - jnp.mean(scaled, axis=-1, keepdims=True)
        - normed * jnp.mean(scaled * normed, axis=-1, keepdims=True)
    )


def gelu_parts(hidden_pre):
    cdf_value = 0.5 * (1.0 + jax.scipy.special.erf(hidden_pre * 2.0 ** (-0.5)))
    density = jnp.exp(-0.5 * hidden_pre * hidden_pre) * (2.0 * math.pi) ** (-0.5)
    return (hidden_pre * cdf_value, cdf_value + hidden_pre * density)


def contract_rows(left, right):
    return lax.dot_general(
        left, right, (((0,), (0,)), ((), ())), preferred_element_type=jnp.float32
    )


def contract_cols(left, right):
    return lax.dot_general(
        left, right, (((1,), (1,)), ((), ())), preferred_element_type=jnp.float32
    )


HEAD_COLS = 3 * HD


def probs_of(packed, head, keep):
    start = head * HEAD_COLS
    query = packed[:, start : start + HD]
    key = packed[:, start + HD : start + 2 * HD]
    value = packed[:, start + 2 * HD : start + 3 * HD]
    scores = jnp.where(keep, contract_cols(key, query) * HD ** (-0.5), -1e30)
    powers = jnp.exp(scores - jnp.max(scores, axis=0, keepdims=True))
    probs = powers * (1.0 / jnp.sum(powers, axis=0, keepdims=True))
    return query, key, value, probs


def forward_kernel(
    tokens, gain, bias, weight, proj_bias, out_mine, out_theirs, low, packed, mixed, mine, theirs
):
    rows = tokens.shape[1]
    _, _, scaled = layer_norm(tokens[0].astype(jnp.float32), gain[...], bias[...])
    low[0] = scaled.astype(jnp.bfloat16)
    projected = jnp.dot(low[0], weight[...], preferred_element_type=jnp.float32)
    packed[0] = (projected + proj_bias[...]).astype(jnp.bfloat16)
    keep = lax.broadcasted_iota(jnp.int32, (rows, rows), 0) < TOK_IMG
    columns = packed[0]
    outs = []
    for head in range(weight.shape[1] // HEAD_COLS):
        _, _, value, probs = probs_of(columns, head, keep)
        outs.append(
            jnp.dot(
                value.astype(jnp.float32).T.astype(jnp.bfloat16),
                probs.astype(jnp.bfloat16),
                preferred_element_type=jnp.float32,
            )
        )
    mixed[0] = jnp.concatenate(outs, axis=0).T.astype(jnp.bfloat16)
    for part, out_weight in ((mine, out_mine), (theirs, out_theirs)):
        part[0] = jnp.dot(
            mixed[0], out_weight[...], preferred_element_type=jnp.float32
        ).astype(jnp.bfloat16)


def backward_kernel(
    packed, upstream, out_weight, back_mine, back_theirs, grad, mine, theirs, query_sum, value_sum
):
    rows = packed.shape[1]
    heads = packed.shape[2] // HEAD_COLS

    @pl.when(pl.program_id(0) == 0)
    def _():
        query_sum[...] = jnp.zeros_like(query_sum)
        value_sum[...] = jnp.zeros_like(value_sum)

    grad_mixed = contract_cols(upstream[0], out_weight[...]).astype(jnp.bfloat16)
    keep = lax.broadcasted_iota(jnp.int32, (rows, rows), 0) < TOK_IMG
    columns = packed[0]
    queries = []
    for head in range(heads):
        query, key, value, probs = probs_of(columns, head, keep)
        grad_head = grad_mixed[:, head * HD : (head + 1) * HD]
        grad_probs = contract_cols(value, grad_head)
        delta = jnp.sum(probs * grad_probs, axis=0, keepdims=True)
        grad_scores = (probs * (grad_probs - delta) * HD ** (-0.5)).astype(jnp.bfloat16)
        grad_value = jnp.dot(
            probs.astype(jnp.bfloat16), grad_head, preferred_element_type=jnp.float32
        )
        grad_key = jnp.dot(grad_scores, query, preferred_element_type=jnp.float32)
        queries.append(
            jnp.dot(
                key.astype(jnp.float32).T.astype(jnp.bfloat16),
                grad_scores,
                preferred_element_type=jnp.float32,
            )
        )
        start = head * HEAD_COLS
        grad[0, :, start + HD : start + 2 * HD] = grad_key.astype(jnp.bfloat16)
        grad[0, :, start + 2 * HD : start + 3 * HD] = grad_value.astype(jnp.bfloat16)
        value_sum[:, head * HD : (head + 1) * HD] += jnp.sum(grad_value, axis=0, keepdims=True)
    grad_query = jnp.concatenate(queries, axis=0).T
    query_sum[...] += jnp.sum(grad_query, axis=0, keepdims=True)
    for head in range(heads):
        start = head * HEAD_COLS
        grad[0, :, start : start + HD] = grad_query[:, head * HD : (head + 1) * HD].astype(
            jnp.bfloat16
        )
    for part, weight in ((mine, back_mine), (theirs, back_theirs)):
        part[0] = contract_cols(grad[0], weight[...]).astype(jnp.bfloat16)


def per_image(shape):
    return pl.BlockSpec((1,) + shape[1:], lambda image: (image, 0, 0))


def resident(shape):
    return pl.BlockSpec(shape, lambda image: (0, 0))


def run_images(kernel, images, args, outs, name):
    spec = lambda shape: per_image(shape) if len(shape) == 3 else resident(shape)
    return pl.pallas_call(
        kernel,
        grid=(images,),
        in_specs=[spec(arg.shape) for arg in args],
        out_specs=[spec(out.shape) for out in outs],
        out_shape=outs,
        compiler_params=pltpu.CompilerParams(vmem_limit_bytes=48 << 20),
        name=name,
    )(*args)


def attention_forward(tokens, gain, bias, weight, proj_bias, out_mine, out_theirs):
    images, rows, features = tokens.shape
    struct = lambda width: jax.ShapeDtypeStruct((images, rows, width), jnp.bfloat16)
    half = out_mine.shape[1]
    outs = [
        struct(features),
        struct(weight.shape[1]),
        struct(out_mine.shape[0]),
        struct(half),
        struct(half),
    ]
    args = (tokens, gain, bias, weight, proj_bias, out_mine, out_theirs)
    return run_images(forward_kernel, images, args, outs, "attention_forward")


def attention_backward(packed, upstream, out_weight, back_mine, back_theirs):
    images, rows, width = packed.shape
    struct = lambda columns: jax.ShapeDtypeStruct((images, rows, columns), jnp.bfloat16)
    sums = jax.ShapeDtypeStruct((1, width // 3), jnp.float32)
    half = back_mine.shape[0]
    outs = [struct(width), struct(half), struct(half), sums, sums]
    args = (packed, upstream, out_weight, back_mine, back_theirs)
    return run_images(backward_kernel, images, args, outs, "attention_backward")


def exchange(block, axis, bit):
    size = lax.axis_size(axis)
    return lax.ppermute(block, axis, [(index, index ^ (1 << bit)) for index in range(size)])


def bit_of(axis, bit):
    return (lax.axis_index(axis) >> bit) % 2 == 1


def bits_in(axis):
    return (lax.axis_size(axis) - 1).bit_length()


def after(value, *others):
    return lax.optimization_barrier((value, *others))[0]


def split_blocks(values, dim):
    count = lax.axis_size("tensor")
    blocks = jnp.split(values, count, axis=dim)
    even = jnp.concatenate(blocks[0::2], axis=dim)
    odd = jnp.concatenate(blocks[1::2], axis=dim)
    upper = bit_of("tensor", 0)
    return jnp.where(upper, odd, even), jnp.where(upper, even, odd)


def join_blocks(mine, theirs):
    count = lax.axis_size("tensor") // 2
    upper = bit_of("tensor", 0)
    pieces = []
    for own, other in zip(jnp.split(mine, count, axis=-1), jnp.split(theirs, count, axis=-1)):
        pieces += [jnp.where(upper, other, own), jnp.where(upper, own, other)]
    return jnp.concatenate(pieces, axis=-1)


def gather_far(block):
    for bit in range(1, bits_in("tensor")):
        got = exchange(block, "tensor", bit)
        upper = bit_of("tensor", bit)
        block = jnp.concatenate(
            [jnp.where(upper, got, block), jnp.where(upper, block, got)], axis=-1
        )
    return block


def gather_near(block):
    return join_blocks(block, exchange(block, "tensor", 0))


def add_near(mine, theirs):
    return mine.astype(jnp.float32) + exchange(theirs, "tensor", 0).astype(jnp.float32)


def add_far(total):
    for bit in range(1, bits_in("tensor")):
        sent = total.astype(jnp.bfloat16)
        total = sent.astype(jnp.float32) + exchange(sent, "tensor", bit).astype(jnp.float32)
    return total.astype(jnp.bfloat16)


def scatter_far(total):
    for bit in reversed(range(1, bits_in("tensor"))):
        low, high = jnp.split(total, 2, axis=-1)
        upper = bit_of("tensor", bit)
        got = exchange(jnp.where(upper, low, high).astype(jnp.bfloat16), "tensor", bit)
        total = jnp.where(upper, high, low) + got.astype(jnp.float32)
    return total


def halve_rows(grad, bit):
    low, high = jnp.split(grad, 2, axis=0)
    upper = bit_of("dp", bit)
    got = exchange(jnp.where(upper, low, high).astype(jnp.bfloat16), "dp", bit)
    return jnp.where(upper, high, low) + got.astype(jnp.float32)


def double_rows(grad, bit):
    got = exchange(grad, "dp", bit)
    upper = bit_of("dp", bit)
    return jnp.concatenate([jnp.where(upper, got, grad), jnp.where(upper, grad, got)], axis=0)


def sum_rows(grad, order):
    for bit in order:
        grad = halve_rows(grad, bit)
    grad = grad.astype(jnp.bfloat16)
    for bit in reversed(order):
        grad = double_rows(grad, bit)
    return grad.astype(jnp.float32)


def sum_small(values, axis):
    packed = jnp.concatenate(values)
    for bit in range(bits_in(axis)):
        packed = packed + exchange(packed, axis, bit)
    result, start = [], 0
    for value in values:
        result.append(packed[start : start + value.shape[0]])
        start += value.shape[0]
    return result


def shards(
    tokens,
    norm1_gain,
    norm1_bias,
    qkv_weight,
    query_bias,
    value_bias,
    out_weight,
    out_bias,
    layer_scale1,
    norm2_gain,
    norm2_bias,
    up_weight,
    up_bias,
    down_weight,
    down_bias,
    layer_scale2,
    cotangent,
):
    images = tokens.shape[0] // TOK_IMG
    width_local = tokens.shape[1]
    features = norm1_gain.shape[0]
    padded = -(-TOK_IMG // 8) * 8
    heads_local = query_bias.shape[0] // HD
    chunks = 2 if images % 2 == 0 else 1
    col_start = lax.axis_index("tensor") * width_local
    order = tuple(range(bits_in("dp")))
    swapped = order[1:2] + order[:1] + order[2:]

    def cols(values):
        return lax.dynamic_slice_in_dim(values, col_start, width_local, values.ndim - 1)

    def pad_rows(values):
        values = values.reshape(images, TOK_IMG, width_local)
        return jnp.pad(values, ((0, 0), (0, padded - TOK_IMG), (0, 0)))

    def flat(values):
        return values.reshape(-1, values.shape[-1])

    def unpad_rows(values):
        values = values.reshape(images, padded, width_local)
        return values[:, :TOK_IMG].reshape(images * TOK_IMG, width_local)

    def in_chunks(values):
        return jnp.split(values, chunks, axis=0)

    def out_of_chunks(values):
        return jnp.concatenate(values, axis=0)

    tokens = pad_rows(tokens)
    cotangent = pad_rows(cotangent)
    out_mine, out_theirs = split_blocks(out_weight, 1)
    qkv_mine, qkv_theirs = split_blocks(qkv_weight, 0)
    up_mine, up_theirs = split_blocks(up_weight, 0)
    down_mine, down_theirs = split_blocks(down_weight, 1)
    proj_bias = jnp.stack(
        [
            query_bias.reshape(heads_local, HD),
            jnp.zeros((heads_local, HD), jnp.float32),
            value_bias.reshape(heads_local, HD),
        ],
        axis=1,
    ).reshape(1, 3 * heads_local * HD)
    tokens_far = [gather_far(part) for part in in_chunks(tokens)]
    scale2_all = gather_near(gather_far(layer_scale2[None]))
    whole = [gather_near(part) for part in tokens_far]
    cotangent_far = gather_far(after(cotangent, *tokens_far))
    upstream_low = gather_near(cotangent_far)

    forward = [
        attention_forward(
            part, norm1_gain[None], norm1_bias[None], qkv_weight, proj_bias, out_mine, out_theirs
        )
        for part in whole
    ]
    upstream = [flat(part) for part in in_chunks(upstream_low)]
    branch_grad = [(part.astype(jnp.float32) * scale2_all).astype(jnp.bfloat16) for part in upstream]

    attended_low, normed2, inv_std2, lowered2, residual = [], [], [], [], []
    activated_low, grad_pre, grad_pre_low = [], [], []
    for index in range(chunks):
        _, _, _, mine, theirs = forward[index]
        total = add_far(add_near(flat(mine), flat(theirs)))
        joined = gather_near(total)
        attended_low.append(joined)
        attended = joined.astype(jnp.float32) + out_bias
        residual.append(flat(whole[index]).astype(jnp.float32) + layer_scale1 * attended)
        normed, inv_std, scaled = layer_norm(residual[index], norm2_gain, norm2_bias)
        normed2.append(normed)
        inv_std2.append(inv_std)
        lowered2.append(scaled.astype(jnp.bfloat16))
        hidden_pre = (
            jnp.dot(lowered2[index], up_weight, preferred_element_type=jnp.float32) + up_bias
        )
        activated, slope = gelu_parts(hidden_pre)
        activated_low.append(activated.astype(jnp.bfloat16))
        grad_pre.append(contract_cols(branch_grad[index], down_weight) * slope)
        grad_pre_low.append(grad_pre[index].astype(jnp.bfloat16))

    lowered2_all = out_of_chunks(lowered2)
    activated_all = out_of_chunks(activated_low)
    grad_pre_all = out_of_chunks(grad_pre_low)
    branch_grad_all = out_of_chunks(branch_grad)
    grad_down_weight = contract_rows(activated_all, branch_grad_all)
    grad_up_weight = contract_rows(lowered2_all, grad_pre_all)
    grad_up_bias = sum(jnp.sum(part, axis=0) for part in grad_pre)

    grad_residual, grad_attended, sums2 = [], [], []
    back = []
    for index in range(chunks):
        total = add_far(
            add_near(
                contract_cols(grad_pre_low[index], up_mine).astype(jnp.bfloat16),
                contract_cols(grad_pre_low[index], up_theirs).astype(jnp.bfloat16),
            )
        )
        grad_lowered2 = gather_near(total).astype(jnp.float32)
        part = upstream[index].astype(jnp.float32) + norm_back(
            grad_lowered2, normed2[index], inv_std2[index], norm2_gain
        )
        grad_residual.append(part)
        attended = attended_low[index].astype(jnp.float32) + out_bias
        sums2.append(
            (
                jnp.sum(grad_lowered2 * normed2[index], axis=0),
                jnp.sum(grad_lowered2, axis=0),
                jnp.sum(part * attended, axis=0),
                jnp.sum(part * layer_scale1, axis=0),
            )
        )
        grad_attended.append((part * layer_scale1).astype(jnp.bfloat16))
        packed = forward[index][1]
        back.append(
            attention_backward(
                packed,
                grad_attended[index].reshape(packed.shape[:2] + (features,)),
                out_weight,
                qkv_mine,
                qkv_theirs,
            )
        )
    grad_norm2_gain, grad_norm2_bias, grad_layer_scale1, grad_out_bias = (
        sum(parts) for parts in zip(*sums2)
    )
    grad_query_bias = sum(parts[3] for parts in back)[0]
    grad_value_bias = sum(parts[4] for parts in back)[0]
    grad_out_weight = contract_rows(
        flat(out_of_chunks([parts[2] for parts in forward])), out_of_chunks(grad_attended)
    )
    grad_qkv_weight = contract_rows(
        flat(out_of_chunks([parts[0] for parts in forward])),
        flat(out_of_chunks([parts[0] for parts in back])),
    )
    grad_lowered1 = out_of_chunks(
        [scatter_far(add_near(flat(parts[1]), flat(parts[2]))) for parts in back]
    )

    branch_cols = (
        scatter_far(
            add_near(
                jnp.dot(
                    activated_all, down_mine, preferred_element_type=jnp.float32
                ).astype(jnp.bfloat16),
                jnp.dot(
                    activated_all, down_theirs, preferred_element_type=jnp.float32
                ).astype(jnp.bfloat16),
            )
        )
        + down_bias
    )
    output = out_of_chunks([cols(part) for part in residual]) + layer_scale2 * branch_cols
    upstream_cols = flat(cotangent).astype(jnp.float32)
    grad_layer_scale2 = jnp.sum(upstream_cols * branch_cols, axis=0)
    grad_down_bias = jnp.sum(upstream_cols * layer_scale2, axis=0)

    tokens_all = flat(out_of_chunks(whole)).astype(jnp.float32)
    row_mean = jnp.mean(tokens_all, axis=-1, keepdims=True)
    centred = tokens_all - row_mean
    inv_std1 = lax.rsqrt(jnp.mean(centred * centred, axis=-1, keepdims=True) + EPS)
    normed1_cols = (flat(tokens).astype(jnp.float32) - row_mean) * inv_std1
    scaled = grad_lowered1 * cols(norm1_gain)
    row_sums = sum_small(
        [jnp.sum(scaled, axis=-1), jnp.sum(scaled * normed1_cols, axis=-1)], "tensor"
    )
    mean_scaled, mean_product = (values[:, None] / features for values in row_sums)
    input_grad = out_of_chunks([cols(part) for part in grad_residual]) + inv_std1 * (
        scaled - mean_scaled - normed1_cols * mean_product
    )

    grad_down_weight = sum_rows(grad_down_weight, order)
    grad_up_weight = sum_rows(grad_up_weight, swapped)
    grad_out_weight = sum_rows(grad_out_weight, order)
    middle = grad_qkv_weight.shape[0] // 2
    grad_qkv_weight = jnp.concatenate(
        [sum_rows(grad_qkv_weight[:middle], order), sum_rows(grad_qkv_weight[middle:], swapped)],
        axis=0,
    )
    small = [
        grad_query_bias,
        grad_value_bias,
        grad_out_bias,
        grad_layer_scale1,
        grad_norm2_gain,
        grad_norm2_bias,
        grad_up_bias,
        grad_down_bias,
        grad_layer_scale2,
    ]
    (
        grad_query_bias,
        grad_value_bias,
        grad_out_bias,
        grad_layer_scale1,
        grad_norm2_gain,
        grad_norm2_bias,
        grad_up_bias,
        grad_down_bias,
        grad_layer_scale2,
    ) = sum_small(small, "dp")
    norm1_sums = jnp.stack(
        sum_small(
            [jnp.sum(grad_lowered1 * normed1_cols, axis=0), jnp.sum(grad_lowered1, axis=0)], "dp"
        )
    )
    grad_norm1_gain, grad_norm1_bias = gather_near(gather_far(norm1_sums))
    output = unpad_rows(output)
    input_grad = unpad_rows(input_grad)
    return (
        output,
        input_grad,
        grad_norm1_gain,
        grad_norm1_bias,
        grad_qkv_weight,
        grad_query_bias,
        grad_value_bias,
        grad_out_weight,
        grad_out_bias,
        grad_layer_scale1,
        grad_norm2_gain,
        grad_norm2_bias,
        grad_up_weight,
        grad_up_bias,
        grad_down_weight,
        grad_down_bias,
        grad_layer_scale2,
    )


def solution(mesh):
    return jax.shard_map(
        shards,
        mesh=mesh,
        in_specs=(
            P("dp", "tensor"),
            P(),
            P(),
            P(None, "tensor"),
            P("tensor"),
            P("tensor"),
            P("tensor", None),
            P(),
            P(),
            P(),
            P(),
            P(None, "tensor"),
            P("tensor"),
            P("tensor", None),
            P("tensor"),
            P("tensor"),
            P("dp", "tensor"),
        ),
        out_specs=(
            P("dp", "tensor"),
            P("dp", "tensor"),
            P(),
            P(),
            P(None, "tensor"),
            P("tensor"),
            P("tensor"),
            P("tensor", None),
            P(),
            P(),
            P(),
            P(),
            P(None, "tensor"),
            P("tensor"),
            P("tensor", None),
            P("tensor"),
            P("tensor"),
        ),
        check_vma=False,
    )
```

time: 816 us -> 405 us (0.50)
  waiting for transfers between devices: 590 us -> 160 us
  starting transfers between devices: 0.32 us -> 60.8 us
  matrix products: 89.5 us -> 29.9 us
  other arithmetic: 36.2 us -> 89 us
  blocking collectives: 39.7 us -> 0 us
  Pallas kernels: 0 us -> 26.2 us
  between operations: 14.7 us -> 3.44 us
  local copies, waits for them, and re-layouts: 40.7 us -> 31.5 us
    psum x4 -> x0, waiting for transfers between devices: 488 us -> none  [the longest x1 358 us: shards(): lax.psum((grad_norm1_gain, grad_norm1_bias, grad_qkv_weight, grad_query_b...]
    ppermute x0 -> x66, waiting for transfers between devices: none -> 160 us  [exchange(): lax.ppermute(block, axis, [(index, index ^ 1 << bit) for index in range(s...]
    all_gather x3 -> x0, waiting for transfers between devices: 68.7 us -> none  [the longest x1 25.7 us: shards(): lax.all_gather(tokens, 'tensor', axis=1, tiled=True).astype(jnp.float32)]
    ppermute x0 -> x66, starting transfers between devices: none -> 60.8 us  [exchange(): lax.ppermute(block, axis, [(index, index ^ 1 << bit) for index in range(s...]
    dot_general x10 -> x4, matrix products: 49.3 us -> 9.35 us  [the longest x2 4.47 us: shards(): jnp.dot(lowered2[index], up_weight, preferred_element_type=jnp.float32)]
    psum x1 -> x0, blocking collectives: 39.7 us -> none  [shards(): lax.psum((grad_norm1_gain, grad_norm1_bias, grad_qkv_weight, grad_query_b...]
    reduce_scatter x1 -> x0, waiting for transfers between devices: 31.7 us -> none  [shards(): lax.psum_scatter(down_part.astype(jnp.bfloat16), 'tensor', scatter_dimens...]
    convert_element_type x2 -> x35, other arithmetic: 2.14 us -> 31.7 us  [the longest x2 9.58 us: shards(): grad_attended.append((part * layer_scale1).astype(jnp.bfloat16))]
  transfers between devices with their start and end apart: 8 -> 66, of which waited for: 8 -> 28; matrix products, arithmetic and copies ran while one was open for 5% -> 25% of each run, Pallas kernels for 0% -> 7%
where the time goes in v2:
time: 405 us; the launch traced here: 401 us
  waiting for transfers between devices  160 us (40%)
  other arithmetic  89 us (22%)
  starting transfers between devices  60.8 us (15%)
  local copies, waits for them, and re-layouts  31.5 us (8%)
  matrix products  29.9 us (7%)
  Pallas kernels  26.2 us (6%)
    ppermute x66, waiting for transfers between devices, exchange(): lax.ppermute(block, axis, [(index, index ^ 1 << bit) for index in range(s...  160 us
    ppermute x66, starting transfers between devices, exchange(): lax.ppermute(block, axis, [(index, index ^ 1 << bit) for index in range(s...  60.8 us
    pallas_call x4, Pallas kernels, run_images(): pl.pallas_call(kernel, grid=(images,), in_specs=[spec(arg.shape) for arg...  26.2 us
    dot_general x6, matrix products, contract_cols(): lax.dot_general(left, right, (((1,), (1,)), ((), ())), preferred_element_...  11.5 us
    convert_element_type x2, other arithmetic, shards(): grad_attended.append((part * layer_scale1).astype(jnp.bfloat16))  9.58 us
    dot_general x4, matrix products, contract_rows(): lax.dot_general(left, right, (((0,), (0,)), ((), ())), preferred_element_...  9.11 us
    unnamed x337, local copies, waits for them, and re-layouts  8.27 us
  transfers between devices with their start and end apart: 66, of which 28 were waited for; matrix products, arithmetic and copies ran while one was open for 25% of the time, Pallas kernels for 7%

profile of v2, /device:TPU:0, one launch (start us, length us, event | category | flops | bytes accessed | tf_op | source)
XLA Modules:
  0.0 400.9 jit_solution(8805323132980049798)
XLA Ops:
  5.6 3.0 fusion.95
  11.5 3.0 fusion.94
  19.9 5.5 %collective-permute-done = bf16[2,264,256]{2,1,0:T(8,128)(2,1)S(1)} collective-permute-done((bf16[2,264,256]{2,1,0:T(8,128)(2,1)S(1)}, bf16[2,264,256]{2,1,0:T(8,128)(2,1)S(1)}, u32[]{:S(2)}, u32[]{:S(2)}) %collective-permute-start) | collective-permute-done | bytes 270368 | tf_op jit(solution)/shard_map/ppermute | solution.py:188
  29.0 6.8 %attention_forward.3 = (bf16[2,264,1024]{2,1,0:T(8,128)(2,1)S(1)}, bf16[2,264,768]{2,1,0:T(8,128)(2,1)S(1)}, bf16[2,264,256]{2,1,0:T(8,128)(2,1)S(1)}, bf16[2,26...) custom-call(bf16[2,264,1024]{2,1,0:T(8,128)(2,1)S(1)} %pad_maximum_fusion.3.tokens, f32[1,1024]{1,0:T(1,128)S(1)} %bitcast.88, ...), custom_call_target="tpu_custom_call" | custom-call | tf_op jit(solution)/shard_map/attention_forward/pallas_call | solution.py:150
  37.0 6.6 %attention_forward.2 = (bf16[2,264,1024]{2,1,0:T(8,128)(2,1)S(1)}, bf16[2,264,768]{2,1,0:T(8,128)(2,1)S(1)}, bf16[2,264,256]{2,1,0:T(8,128)(2,1)S(1)}, bf16[2,26...) custom-call(bf16[2,264,1024]{2,1,0:T(8,128)(2,1)S(1)} %pad_maximum_fusion.2.tokens, f32[1,1024]{1,0:T(1,128)S(1)} %bitcast.89, ...), custom_call_target="tpu_custom_call" | custom-call | tf_op jit(solution)/shard_map/attention_forward/pallas_call | solution.py:150
  47.5 12.8 %collective-permute-done.8 = bf16[528,512]{1,0:T(8,128)(2,1)S(1)} collective-permute-done((bf16[528,512]{1,0:T(8,128)(2,1)S(1)}, bf16[528,512]{1,0:T(8,128)(2,1)S(1)}, u32[]{:S(2)}, u32[]{:S(2)}) %collective-permute-start.8) | collective-permute-done | bytes 540704 | tf_op jit(solution)/shard_map/ppermute | solution.py:188
  60.5 11.0 %collective-permute-done.3 = bf16[528,512]{1,0:T(8,128)(2,1)S(1)} collective-permute-done((bf16[528,512]{1,0:T(8,128)(2,1)S(1)}, bf16[528,512]{1,0:T(8,128)(2,1)S(1)}, u32[]{:S(2)}, u32[]{:S(2)}) %collective-permute-start.3) | collective-permute-done | bytes 540704 | tf_op jit(solution)/shard_map/ppermute | solution.py:188
  79.5 3.4 add_convert_fusion.1
  95.9 13.7 %collective-permute-done.17 = bf16[528,512]{1,0:T(8,128)(2,1)} collective-permute-done((bf16[528,512]{1,0:T(8,128)(2,1)}, bf16[528,512]{1,0:T(8,128)(2,1)}, u32[]{:S(2)}, u32[]{:S(2)}) %collective-permute-start.17) | collective-permute-done | bytes 540704 | tf_op jit(solution)/shard_map/ppermute | solution.py:188
  115.7 3.6 convert_reduce_fusion.2
  119.4 3.2 multiply_convert_fusion.3
  130.6 2.9 fusion.52
  151.1 12.5 %collective-permute-done.54 = bf16[512,1024]{1,0:T(8,128)(2,1)} collective-permute-done((bf16[512,1024]{1,0:T(8,128)(2,1)}, bf16[512,1024]{1,0:T(8,128)(2,1)}, u32[]{:S(2)}, u32[]{:S(2)}) %collective-permute-start.54) | collective-permute-done | bytes 1048608 | tf_op jit(solution)/shard_map/ppermute | solution.py:188
  174.6 5.2 %collective-permute-done.55 = bf16[256,1024]{1,0:T(8,128)(2,1)S(1)} collective-permute-done((bf16[256,1024]{1,0:T(8,128)(2,1)S(1)}, bf16[256,1024]{1,0:T(8,128)(2,1)S(1)}, u32[]{:S(2)}, u32[]{:S(2)}) %collective-permute-start.55) | collective-permute-done | bytes 524320 | tf_op jit(solution)/shard_map/ppermute | solution.py:188
  194.9 5.7 %multiply_convert_fusion.1 = (bf16[528,1024]{1,0:T(8,128)(2,1)}, f32[528,1024]{1,0:T(8,128)}, f32[528]{0:T(1024)S(1)}, f32[1024]{0:T(1024)}) fusion(f32[1024]{0:T(1024)S(1)} %copy-done.117, f32[528]{0:T(1024)} %div.60, f32[528,1024]{1,0:T(8,128)} %get-tuple-element.87, f32[528]{0:T(1024)S(1)} %div.53, f32[528]{0:T(1024)S(1)} %broadcast_multiply_fusion.3, ...), kind=kLoop, calls=%fused_computation.80 | loop fusion | flops 16218608 | bytes 8673600 | tf_op jit(solution)/shard_map/convert_element_type | solution.py:418
  201.5 3.9 multiply_convert_fusion
  206.5 5.0 %multiply_reduce_fusion.1 = (f32[1024]{0:T(1024)S(1)}, f32[1024]{0:T(1024)S(1)}, f32[1024]{0:T(1024)S(1)}, f32[1024]{0:T(1024)S(1)}, f32[2,264,1024]{2,1,0:T(8,128)S(1)}, /*index=5*/f32[2,264,1024]{2,1,0:T(8,128)S(1)}) fusion(f32[1024]{0:T(1024)S(1)} %copy-done.140, bf16[2,264,256]{2,1,0:T(8,128)(2,1)S(1)} %bitcast.135, ...), kind=kLoop, calls=%fused_computation.82 | loop fusion | flops 43249664 | bytes 13021696 | tf_op jit(solution)/shard_map/reduce_sum | solution.py:414
  212.8 6.3 %attention_backward.3 = (bf16[2,264,768]{2,1,0:T(8,128)(2,1)S(1)}, bf16[2,264,512]{2,1,0:T(8,128)(2,1)S(1)}, bf16[2,264,512]{2,1,0:T(8,128)(2,1)S(1)}, f32[1,256]{1,0:T(1,128)S(1)}, f32[1,256]{1,0:T(1,128)S(1)}) custom-call(bf16[2,264,768]{2,1,0:T(8,128)(2,1)S(1)} %get-tuple-element.46.packed, bf16[2,264,1024]{2,1,0:T(8,128)(2,1)S(1)} %get-tuple-element.215.upstream, ...), custom_call_target="tpu_custom_call" | custom-call | tf_op jit(solution)/shard_map/attention_backward/pallas_call | solution.py:150
  219.2 6.5 %attention_backward.2 = (bf16[2,264,768]{2,1,0:T(8,128)(2,1)S(1)}, bf16[2,264,512]{2,1,0:T(8,128)(2,1)S(1)}, bf16[2,264,512]{2,1,0:T(8,128)(2,1)S(1)}, f32[1,256]{1,0:T(1,128)S(1)}, f32[1,256]{1,0:T(1,128)S(1)}) custom-call(bf16[2,264,768]{2,1,0:T(8,128)(2,1)S(1)} %copy-done.2, bf16[2,264,1024]{2,1,0:T(8,128)(2,1)S(1)} %get-tuple-element.214.upstream, ...), custom_call_target="tpu_custom_call" | custom-call | tf_op jit(solution)/shard_map/attention_backward/pallas_call | solution.py:150
  248.2 8.3 %collective-permute-done.48 = bf16[128,1024]{1,0:T(8,128)(2,1)S(1)} collective-permute-done((bf16[128,1024]{1,0:T(8,128)(2,1)S(1)}, bf16[128,1024]{1,0:T(8,128)(2,1)S(1)}, u32[]{:S(2)}, u32[]{:S(2)}) %collective-permute-start.48) | collective-permute-done | bytes 262176 | tf_op jit(solution)/shard_map/ppermute | solution.py:188
  260.4 9.4 %collective-permute-done.49 = bf16[64,1024]{1,0:T(8,128)(2,1)S(1)} collective-permute-done((bf16[64,1024]{1,0:T(8,128)(2,1)S(1)}, bf16[64,1024]{1,0:T(8,128)(2,1)S(1)}, u32[]{:S(2)}, u32[]{:S(2)}) %collective-permute-start.49) | collective-permute-done | bytes 131104 | tf_op jit(solution)/shard_map/ppermute | solution.py:188
  271.3 10.4 %collective-permute-done.50 = bf16[32,1024]{1,0:T(8,128)(2,1)S(1)} collective-permute-done((bf16[32,1024]{1,0:T(8,128)(2,1)S(1)}, bf16[32,1024]{1,0:T(8,128)(2,1)S(1)}, u32[]{:S(2)}, u32[]{:S(2)}) %collective-permute-start.50) | collective-permute-done | bytes 65568 | tf_op jit(solution)/shard_map/ppermute | solution.py:188
  295.2 10.2 %collective-permute-done.52 = bf16[64,1024]{1,0:T(8,128)(2,1)S(1)} collective-permute-done((bf16[64,1024]{1,0:T(8,128)(2,1)S(1)}, bf16[64,1024]{1,0:T(8,128)(2,1)S(1)}, u32[]{:S(2)}, u32[]{:S(2)}) %collective-permute-start.52) | collective-permute-done | bytes 131104 | tf_op jit(solution)/shard_map/ppermute | solution.py:188
  305.4 3.8 collective-permute-start.41
  310.0 4.2 %collective-permute-done.41 = bf16[64,768]{1,0:T(8,128)(2,1)S(1)} collective-permute-done((bf16[64,768]{1,0:T(8,128)(2,1)S(1)}, bf16[64,768]{1,0:T(8,128)(2,1)S(1)}, u32[]{:S(2)}, u32[]{:S(2)}) %collective-permute-start.41) | collective-permute-done | bytes 98336 | tf_op jit(solution)/shard_map/ppermute | solution.py:188
  315.4 6.0 %collective-permute-done.35 = bf16[64,768]{1,0:T(8,128)(2,1)S(1)} collective-permute-done((bf16[64,768]{1,0:T(8,128)(2,1)S(1)}, bf16[64,768]{1,0:T(8,128)(2,1)S(1)}, u32[]{:S(2)}, u32[]{:S(2)}) %collective-permute-start.35) | collective-permute-done | bytes 98336 | tf_op jit(solution)/shard_map/ppermute | solution.py:188
  321.4 5.7 %collective-permute-done.42 = bf16[64,768]{1,0:T(8,128)(2,1)S(1)} collective-permute-done((bf16[64,768]{1,0:T(8,128)(2,1)S(1)}, bf16[64,768]{1,0:T(8,128)(2,1)S(1)}, u32[]{:S(2)}, u32[]{:S(2)}) %collective-permute-start.42) | collective-permute-done | bytes 98336 | tf_op jit(solution)/shard_map/ppermute | solution.py:188
  335.6 3.5 collective-permute-done.29
  344.3 3.0 collective-permute-done.31
  370.1 4.0 collective-permute-done.44
  374.2 3.0 collective-permute-done.38
  379.3 15.3 %collective-permute-done.59 = bf16[512,1024]{1,0:T(8,128)(2,1)S(1)} collective-permute-done((bf16[512,1024]{1,0:T(8,128)(2,1)S(1)}, bf16[512,1024]{1,0:T(8,128)(2,1)S(1)}, u32[]{:S(2)}, u32[]{:S(2)}) %collective-permute-start.59) | collective-permute-done | bytes 1048608 | tf_op jit(solution)/shard_map/ppermute | solution.py:188
  (638 shorter events, 190.2 us)
Async XLA Ops:
  2.6 13.7 %collective-permute-start.5 = (bf16[2,264,256]{2,1,0:T(8,128)(2,1)}, bf16[2,264,256]{2,1,0:T(8,128)(2,1)}, u32[]{:S(2)}, u32[]{:S(2)}) collective-permute-start(bf16[2,264,256]{2,1,0:T(8,128)(2,1)} %pad_slice_fusion), channel_id=1, source_target_pairs={{0,2},{1,3},{2,0},{3,1},{4,6},{5,7},{6,4},{7,5},{8,10},{9,11},{10,... | collective-permute-start | bytes 811016 | tf_op jit(solution)/shard_map/ppermute | solution.py:188
  5.6 20.1 %collective-permute-start.14 = (f32[1,256]{1,0:T(1,128)}, f32[1,256]{1,0:T(1,128)S(1)}, u32[]{:S(2)}, u32[]{:S(2)}) collective-permute-start(f32[1,256]{1,0:T(1,128)} %bitcast.168), channel_id=1, source_target_pairs={{0,2},{1,3},{2,0},{3,1},{4,6},{5,7},{6,4},{7,5},{8,10},{9,11},{10,... | collective-permute-start | bytes 3080 | tf_op jit(solution)/shard_map/ppermute | solution.py:188
  25.7 21.8 %collective-permute-start.15 = (f32[1,512]{1,0:T(1,128)S(1)}, f32[1,512]{1,0:T(1,128)S(1)}, u32[]{:S(2)}, u32[]{:S(2)}) collective-permute-start(f32[1,512]{1,0:T(1,128)S(1)} %pad_maximum_fusion.46), channel_id=1, source_target_pairs={{0,1},{1,0},{2,3},{3,2},{4,5},{5,4},{6,7},{7,6},{8,9},{9,8},{10,11... | collective-permute-start | bytes 6152 | tf_op jit(solution)/shard_map/ppermute | solution.py:188
  26.2 17.5 %collective-permute-start.12 = (bf16[4,264,256]{2,1,0:T(8,128)(2,1)S(1)}, bf16[4,264,256]{2,1,0:T(8,128)(2,1)S(1)}, u32[]{:S(2)}, u32[]{:S(2)}) collective-permute-start(bf16[4,264,256]{2,1,0:T(8,128)(2,1)S(1)} %copy-done.96), channel_id=1, source_target_pairs={{0,2},{1,3},{2,0},{3,1},{4,6},{5,7},{6,4},{7,5},{8,10},{9,11},{10,... | collective-permute-start | bytes 1622024 | tf_op jit(solution)/shard_map/ppermute | solution.py:188
  45.0 26.8 %collective-permute-start.13 = (bf16[4,264,512]{2,1,0:T(8,128)(2,1)S(1)}, bf16[4,264,512]{2,1,0:T(8,128)(2,1)S(1)}, u32[]{:S(2)}, u32[]{:S(2)}) collective-permute-start(bf16[4,264,512]{2,1,0:T(8,128)(2,1)S(1)} %pad_maximum_fusion.6), channel_id=1, source_target_pairs={{0,1},{1,0},{2,3},{3,2},{4,5},{5,4},{6,7},{7,6},{8,9},{9,8},{10,11... | collective-permute-start | bytes 3244040 | tf_op jit(solution)/shard_map/ppermute | solution.py:188
  45.2 15.1 %collective-permute-start.8 = (bf16[528,512]{1,0:T(8,128)(2,1)S(1)}, bf16[528,512]{1,0:T(8,128)(2,1)S(1)}, u32[]{:S(2)}, u32[]{:S(2)}) collective-permute-start(bf16[528,512]{1,0:T(8,128)(2,1)S(1)} %fusion.68), channel_id=1, source_target_pairs={{0,2},{1,3},{2,0},{3,1},{4,6},{5,7},{6,4},{7,5},{8,10},{9,11},{10,... | collective-permute-start | bytes 1622024 | tf_op jit(solution)/shard_map/ppermute | solution.py:188
  45.9 25.6 %collective-permute-start.3 = (bf16[528,512]{1,0:T(8,128)(2,1)S(1)}, bf16[528,512]{1,0:T(8,128)(2,1)S(1)}, u32[]{:S(2)}, u32[]{:S(2)}) collective-permute-start(bf16[528,512]{1,0:T(8,128)(2,1)S(1)} %fusion.69), channel_id=1, source_target_pairs={{0,2},{1,3},{2,0},{3,1},{4,6},{5,7},{6,4},{7,5},{8,10},{9,11},{10,... | collective-permute-start | bytes 1622024 | tf_op jit(solution)/shard_map/ppermute | solution.py:188
  60.5 13.8 %collective-permute-start.9 = (bf16[528,512]{1,0:T(8,128)(2,1)S(1)}, bf16[528,512]{1,0:T(8,128)(2,1)S(1)}, u32[]{:S(2)}, u32[]{:S(2)}) collective-permute-start(bf16[528,512]{1,0:T(8,128)(2,1)S(1)} %add_convert_fusion.6), channel_id=1, source_target_pairs={{0,1},{1,0},{2,3},{3,2},{4,5},{5,4},{6,7},{7,6},{8,9},{9,8},{10,11... | collective-permute-start | bytes 1622024 | tf_op jit(solution)/shard_map/ppermute | solution.py:188
  94.6 15.0 %collective-permute-start.17 = (bf16[528,512]{1,0:T(8,128)(2,1)}, bf16[528,512]{1,0:T(8,128)(2,1)}, u32[]{:S(2)}, u32[]{:S(2)}) collective-permute-start(bf16[528,512]{1,0:T(8,128)(2,1)} %add_convert_fusion.5), channel_id=1, source_target_pairs={{0,2},{1,3},{2,0},{3,1},{4,6},{5,7},{6,4},{7,5},{8,10},{9,11},{10,... | collective-permute-start | bytes 1622024 | tf_op jit(solution)/shard_map/ppermute | solution.py:188
  135.9 34.3 %collective-permute-start.10 = (bf16[1056,512]{1,0:T(8,128)(2,1)}, bf16[1056,512]{1,0:T(8,128)(2,1)}, u32[]{:S(2)}, u32[]{:S(2)}) collective-permute-start(bf16[1056,512]{1,0:T(8,128)(2,1)} %convolution_convert_fusion), channel_id=1, source_target_pairs={{0,1},{1,0},{2,3},{3,2},{4,5},{5,4},{6,7},{7,6},{8,9},{9,8},{10,11... | collective-permute-start | bytes 3244040 | tf_op jit(solution)/shard_map/ppermute | solution.py:188
  137.7 25.9 %collective-permute-start.54 = (bf16[512,1024]{1,0:T(8,128)(2,1)}, bf16[512,1024]{1,0:T(8,128)(2,1)}, u32[]{:S(2)}, u32[]{:S(2)}) collective-permute-start(bf16[512,1024]{1,0:T(8,128)(2,1)} %select_convert_fusion.1), channel_id=1, source_target_pairs={{0,8},{4,12},{8,0},{12,4},{16,24},{20,28},{24,16},{28,20},{1,9},{5... | collective-permute-start | bytes 3145736 | tf_op jit(solution)/shard_map/ppermute | solution.py:188
  143.0 25.8 %collective-permute-start.60 = (bf16[512,1024]{1,0:T(8,128)(2,1)}, bf16[512,1024]{1,0:T(8,128)(2,1)S(1)}, u32[]{:S(2)}, u32[]{:S(2)}) collective-permute-start(bf16[512,1024]{1,0:T(8,128)(2,1)} %select_convert_fusion), channel_id=1, source_target_pairs={{0,4},{4,0},{8,12},{12,8},{16,20},{20,16},{24,28},{28,24},{1,5},{5... | collective-permute-start | bytes 3145736 | tf_op jit(solution)/shard_map/ppermute | solution.py:188
  150.5 23.1 %collective-permute-start.20 = (bf16[528,512]{1,0:T(8,128)(2,1)S(1)}, bf16[528,512]{1,0:T(8,128)(2,1)S(1)}, u32[]{:S(2)}, u32[]{:S(2)}) collective-permute-start(bf16[528,512]{1,0:T(8,128)(2,1)S(1)} %add_convert_fusion.3), channel_id=1, source_target_pairs={{0,2},{1,3},{2,0},{3,1},{4,6},{5,7},{6,4},{7,5},{8,10},{9,11},{10,... | collective-permute-start | bytes 1622024 | tf_op jit(solution)/shard_map/ppermute | solution.py:188
  165.9 13.9 %collective-permute-start.55 = (bf16[256,1024]{1,0:T(8,128)(2,1)S(1)}, bf16[256,1024]{1,0:T(8,128)(2,1)S(1)}, u32[]{:S(2)}, u32[]{:S(2)}) collective-permute-start(bf16[256,1024]{1,0:T(8,128)(2,1)S(1)} %select_convert_fusion.4), channel_id=1, source_target_pairs={{0,4},{4,0},{8,12},{12,8},{16,20},{20,16},{24,28},{28,24},{1,5},{5... | collective-permute-start | bytes 1572872 | tf_op jit(solution)/shard_map/ppermute | solution.py:188
  169.7 13.8 %collective-permute-start.61 = (bf16[256,1024]{1,0:T(8,128)(2,1)S(1)}, bf16[256,1024]{1,0:T(8,128)(2,1)S(1)}, u32[]{:S(2)}, u32[]{:S(2)}) collective-permute-start(bf16[256,1024]{1,0:T(8,128)(2,1)S(1)} %select_convert_fusion.3), channel_id=1, source_target_pairs={{0,8},{4,12},{8,0},{12,4},{16,24},{20,28},{24,16},{28,20},{1,9},{5... | collective-permute-start | bytes 1572872 | tf_op jit(solution)/shard_map/ppermute | solution.py:188
  173.0 14.1 %collective-permute-start.11 = (bf16[1056,256]{1,0:T(8,128)(2,1)S(1)}, bf16[1056,256]{1,0:T(8,128)(2,1)S(1)}, u32[]{:S(2)}, u32[]{:S(2)}) collective-permute-start(bf16[1056,256]{1,0:T(8,128)(2,1)S(1)} %select_convert_fusion.2), channel_id=1, source_target_pairs={{0,2},{1,3},{2,0},{3,1},{4,6},{5,7},{6,4},{7,5},{8,10},{9,11},{10,... | collective-permute-start | bytes 1622024 | tf_op jit(solution)/shard_map/ppermute | solution.py:188
  174.5 16.9 %collective-permute-start.21 = (bf16[528,512]{1,0:T(8,128)(2,1)}, bf16[528,512]{1,0:T(8,128)(2,1)}, u32[]{:S(2)}, u32[]{:S(2)}) collective-permute-start(bf16[528,512]{1,0:T(8,128)(2,1)} %add_convert_fusion.2), channel_id=1, source_target_pairs={{0,1},{1,0},{2,3},{3,2},{4,5},{5,4},{6,7},{7,6},{8,9},{9,8},{10,11... | collective-permute-start | bytes 1622024 | tf_op jit(solution)/shard_map/ppermute | solution.py:188
  180.8 64.0 %collective-permute-start.56 = (bf16[128,1024]{1,0:T(8,128)(2,1)}, bf16[128,1024]{1,0:T(8,128)(2,1)}, u32[]{:S(2)}, u32[]{:S(2)}) collective-permute-start(bf16[128,1024]{1,0:T(8,128)(2,1)} %select_convert_fusion.10), channel_id=1, source_target_pairs={{0,16},{4,20},{8,24},{12,28},{16,0},{20,4},{24,8},{28,12},{1,17},{... | collective-permute-start | bytes 786440 | tf_op jit(solution)/shard_map/ppermute | solution.py:188
  184.8 61.9 %collective-permute-start.62 = (bf16[128,1024]{1,0:T(8,128)(2,1)}, bf16[128,1024]{1,0:T(8,128)(2,1)}, u32[]{:S(2)}, u32[]{:S(2)}) collective-permute-start(bf16[128,1024]{1,0:T(8,128)(2,1)} %select_convert_fusion.9), channel_id=1, source_target_pairs={{0,16},{4,20},{8,24},{12,28},{16,0},{20,4},{24,8},{28,12},{1,17},{... | collective-permute-start | bytes 786440 | tf_op jit(solution)/shard_map/ppermute | solution.py:188
  219.1 70.6 %collective-permute-start.24 = (bf16[528,512]{1,0:T(8,128)(2,1)S(1)}, bf16[528,512]{1,0:T(8,128)(2,1)S(1)}, u32[]{:S(2)}, u32[]{:S(2)}) collective-permute-start(bf16[528,512]{1,0:T(8,128)(2,1)S(1)} %bitcast.93), channel_id=1, source_target_pairs={{0,1},{1,0},{2,3},{3,2},{4,5},{5,4},{6,7},{7,6},{8,9},{9,8},{10,11... | collective-permute-start | bytes 1622024 | tf_op jit(solution)/shard_map/ppermute | solution.py:188
  225.7 66.7 %collective-permute-start.22 = (bf16[528,512]{1,0:T(8,128)(2,1)S(1)}, bf16[528,512]{1,0:T(8,128)(2,1)S(1)}, u32[]{:S(2)}, u32[]{:S(2)}) collective-permute-start(bf16[528,512]{1,0:T(8,128)(2,1)S(1)} %bitcast.92), channel_id=1, source_target_pairs={{0,1},{1,0},{2,3},{3,2},{4,5},{5,4},{6,7},{7,6},{8,9},{9,8},{10,11... | collective-permute-start | bytes 1622024 | tf_op jit(solution)/shard_map/ppermute | solution.py:188
  242.3 16.1 %collective-permute-start.33 = (bf16[256,768]{1,0:T(8,128)(2,1)S(1)}, bf16[256,768]{1,0:T(8,128)(2,1)S(1)}, u32[]{:S(2)}, u32[]{:S(2)}) collective-permute-start(bf16[256,768]{1,0:T(8,128)(2,1)S(1)} %get-tuple-element.92), channel_id=1, source_target_pairs={{0,4},{4,0},{8,12},{12,8},{16,20},{20,16},{24,28},{28,24},{1,5},{5... | collective-permute-start | bytes 1179656 | tf_op jit(solution)/shard_map/ppermute | solution.py:188
  256.4 25.2 %collective-permute-start.57 = (bf16[128,1024]{1,0:T(8,128)(2,1)S(1)}, bf16[128,1024]{1,0:T(8,128)(2,1)S(1)}, u32[]{:S(2)}, u32[]{:S(2)}) collective-permute-start(bf16[128,1024]{1,0:T(8,128)(2,1)S(1)} %add_convert_fusion.9), channel_id=1, source_target_pairs={{0,16},{4,20},{8,24},{12,28},{16,0},{20,4},{24,8},{28,12},{1,17},{... | collective-permute-start | bytes 786440 | tf_op jit(solution)/shard_map/ppermute | solution.py:188
  258.5 23.3 %collective-permute-start.63 = (bf16[128,1024]{1,0:T(8,128)(2,1)S(1)}, bf16[128,1024]{1,0:T(8,128)(2,1)S(1)}, u32[]{:S(2)}, u32[]{:S(2)}) collective-permute-start(bf16[128,1024]{1,0:T(8,128)(2,1)S(1)} %add_convert_fusion.8), channel_id=1, source_target_pairs={{0,16},{4,20},{8,24},{12,28},{16,0},{20,4},{24,8},{28,12},{1,17},{... | collective-permute-start | bytes 786440 | tf_op jit(solution)/shard_map/ppermute | solution.py:188
  287.8 78.9 %collective-permute-start.58 = (bf16[256,1024]{1,0:T(8,128)(2,1)}, bf16[256,1024]{1,0:T(8,128)(2,1)}, u32[]{:S(2)}, u32[]{:S(2)}) collective-permute-start(bf16[256,1024]{1,0:T(8,128)(2,1)} %pad_maximum_fusion.31), channel_id=1, source_target_pairs={{0,4},{4,0},{8,12},{12,8},{16,20},{20,16},{24,28},{28,24},{1,5},{5... | collective-permute-start | bytes 1572872 | tf_op jit(solution)/shard_map/ppermute | solution.py:188
  289.7 78.4 %collective-permute-start.64 = (bf16[256,1024]{1,0:T(8,128)(2,1)}, bf16[256,1024]{1,0:T(8,128)(2,1)}, u32[]{:S(2)}, u32[]{:S(2)}) collective-permute-start(bf16[256,1024]{1,0:T(8,128)(2,1)} %pad_maximum_fusion.32), channel_id=1, source_target_pairs={{0,8},{4,12},{8,0},{12,4},{16,24},{20,28},{24,16},{28,20},{1,9},{5... | collective-permute-start | bytes 1572872 | tf_op jit(solution)/shard_map/ppermute | solution.py:188
  292.8 34.4 %collective-permute-start.25 = (bf16[528,256]{1,0:T(8,128)(2,1)S(1)}, bf16[528,256]{1,0:T(8,128)(2,1)S(1)}, u32[]{:S(2)}, u32[]{:S(2)}) collective-permute-start(bf16[528,256]{1,0:T(8,128)(2,1)S(1)} %select_convert_fusion.7), channel_id=1, source_target_pairs={{0,2},{1,3},{2,0},{3,1},{4,6},{5,7},{6,4},{7,5},{8,10},{9,11},{10,... | collective-permute-start | bytes 811016 | tf_op jit(solution)/shard_map/ppermute | solution.py:188
  293.6 34.1 %collective-permute-start.23 = (bf16[528,256]{1,0:T(8,128)(2,1)S(1)}, bf16[528,256]{1,0:T(8,128)(2,1)S(1)}, u32[]{:S(2)}, u32[]{:S(2)}) collective-permute-start(bf16[528,256]{1,0:T(8,128)(2,1)S(1)} %select_convert_fusion.8), channel_id=1, source_target_pairs={{0,2},{1,3},{2,0},{3,1},{4,6},{5,7},{6,4},{7,5},{8,10},{9,11},{10,... | collective-permute-start | bytes 811016 | tf_op jit(solution)/shard_map/ppermute | solution.py:188
  327.2 31.5 %collective-permute-start.53 = (bf16[128,1024]{1,0:T(8,128)(2,1)}, bf16[128,1024]{1,0:T(8,128)(2,1)}, u32[]{:S(2)}, u32[]{:S(2)}) collective-permute-start(bf16[128,1024]{1,0:T(8,128)(2,1)} %pad_maximum_fusion.37), channel_id=1, source_target_pairs={{0,4},{4,0},{8,12},{12,8},{16,20},{20,16},{24,28},{28,24},{1,5},{5... | collective-permute-start | bytes 786440 | tf_op jit(solution)/shard_map/ppermute | solution.py:188
  334.9 26.1 %collective-permute-start.43 = (bf16[128,768]{1,0:T(8,128)(2,1)}, bf16[128,768]{1,0:T(8,128)(2,1)}, u32[]{:S(2)}, u32[]{:S(2)}) collective-permute-start(bf16[128,768]{1,0:T(8,128)(2,1)} %pad_maximum_fusion.39), channel_id=1, source_target_pairs={{0,4},{4,0},{8,12},{12,8},{16,20},{20,16},{24,28},{28,24},{1,5},{5... | collective-permute-start | bytes 589832 | tf_op jit(solution)/shard_map/ppermute | solution.py:188
  368.0 26.6 %collective-permute-start.59 = (bf16[512,1024]{1,0:T(8,128)(2,1)S(1)}, bf16[512,1024]{1,0:T(8,128)(2,1)S(1)}, u32[]{:S(2)}, u32[]{:S(2)}) collective-permute-start(bf16[512,1024]{1,0:T(8,128)(2,1)S(1)} %pad_maximum_fusion.17), channel_id=1, source_target_pairs={{0,8},{4,12},{8,0},{12,4},{16,24},{20,28},{24,16},{28,20},{1,9},{5... | collective-permute-start | bytes 3145736 | tf_op jit(solution)/shard_map/ppermute | solution.py:188
  369.5 28.1 %collective-permute-start.65 = (bf16[512,1024]{1,0:T(8,128)(2,1)S(1)}, bf16[512,1024]{1,0:T(8,128)(2,1)S(1)}, u32[]{:S(2)}, u32[]{:S(2)}) collective-permute-start(bf16[512,1024]{1,0:T(8,128)(2,1)S(1)} %pad_maximum_fusion.18), channel_id=1, source_target_pairs={{0,4},{4,0},{8,12},{12,8},{16,20},{20,16},{24,28},{28,24},{1,5},{5... | collective-permute-start | bytes 3145736 | tf_op jit(solution)/shard_map/ppermute | solution.py:188
  (201 other events, 1142.1 us)

commit v3 on v2

--- a/solution.py
+++ b/solution.py
@@ -50,6 +50,7 @@
 
 
 HEAD_COLS = 3 * HD
+VMEM_BYTES = 48 << 20
 
 
 def probs_of(packed, head, keep):
@@ -91,7 +92,9 @@
 
 
 def backward_kernel(
-    packed, upstream, out_weight, back_mine, back_theirs, grad, mine, theirs, query_sum, value_sum
+    core, tokens, attended_low, low2_mine, low2_theirs, cotangent, vectors, packed, out_weight,
+    back_mine, back_theirs, residual_grad, upstream, grad, mine, theirs, query_sum, value_sum,
+    feature_sums,
 ):
     rows = packed.shape[1]
     heads = packed.shape[2] // HEAD_COLS
@@ -100,7 +103,22 @@
     def _():
         query_sum[...] = jnp.zeros_like(query_sum)
         value_sum[...] = jnp.zeros_like(value_sum)
-
+        feature_sums[...] = jnp.zeros_like(feature_sums)
+
+    attended = attended_low[0].astype(jnp.float32) + vectors[0:1]
+    residual = tokens[0].astype(jnp.float32) + vectors[1:2] * attended
+    normed, inv_std, _ = layer_norm(residual, vectors[2:3], vectors[3:4])
+    grad_low2 = rejoin(core[0] == 1, low2_mine, low2_theirs)
+    grad_residual = cotangent[0].astype(jnp.float32) + norm_back(
+        grad_low2, normed, inv_std, vectors[2:3]
+    )
+    residual_grad[0] = grad_residual
+    grad_attended = grad_residual * vectors[1:2]
+    upstream[0] = grad_attended.astype(jnp.bfloat16)
+    for row, product in enumerate(
+        (grad_low2 * normed, grad_low2, grad_residual * attended, grad_attended)
+    ):
+        feature_sums[row : row + 1] += jnp.sum(product, axis=0, keepdims=True)
     grad_mixed = contract_cols(upstream[0], out_weight[...]).astype(jnp.bfloat16)
     keep = lax.broadcasted_iota(jnp.int32, (rows, rows), 0) < TOK_IMG
     columns = packed[0]
@@ -137,6 +155,38 @@
         part[0] = contract_cols(grad[0], weight[...]).astype(jnp.bfloat16)
 
 
+def rejoin(upper, mine, theirs):
+    own, other = mine[0].astype(jnp.float32), theirs[0].astype(jnp.float32)
+    return jnp.concatenate(
+        [jnp.where(upper, other, own), jnp.where(upper, own, other)], axis=-1
+    )
+
+
+def hidden_kernel(
+    core, tokens, mine, theirs, upstream, vectors, up_weight, up_bias, down_weight, up_mine,
+    up_theirs, attended_low, low, activated_low, branch_grad, grad_low, part_mine, part_theirs,
+    bias_sum,
+):
+    @pl.when(pl.program_id(0) == 0)
+    def _():
+        bias_sum[...] = jnp.zeros_like(bias_sum)
+
+    joined = rejoin(core[0] == 1, mine, theirs)
+    attended_low[0] = joined.astype(jnp.bfloat16)
+    residual = tokens[0].astype(jnp.float32) + vectors[1:2] * (joined + vectors[0:1])
+    _, _, scaled = layer_norm(residual, vectors[2:3], vectors[3:4])
+    low[0] = scaled.astype(jnp.bfloat16)
+    branch_grad[0] = (upstream[0].astype(jnp.float32) * vectors[4:5]).astype(jnp.bfloat16)
+    hidden_pre = jnp.dot(low[0], up_weight[...], preferred_element_type=jnp.float32) + up_bias[...]
+    activated, slope = gelu_parts(hidden_pre)
+    activated_low[0] = activated.astype(jnp.bfloat16)
+    grad_pre = contract_cols(branch_grad[0], down_weight[...]) * slope
+    bias_sum[...] += jnp.sum(grad_pre, axis=0, keepdims=True)
+    grad_low[0] = grad_pre.astype(jnp.bfloat16)
+    for part, weight in ((part_mine, up_mine), (part_theirs, up_theirs)):
+        part[0] = contract_cols(grad_low[0], weight[...]).astype(jnp.bfloat16)
+
+
 def per_image(shape):
     return pl.BlockSpec((1,) + shape[1:], lambda image: (image, 0, 0))
 
@@ -145,42 +195,55 @@
     return pl.BlockSpec(shape, lambda image: (0, 0))
 
 
-def run_images(kernel, images, args, outs, name):
+def run_images(kernel, args, outs, name, core=None):
+    images = next(arg.shape[0] for arg in args if arg.ndim == 3)
     spec = lambda shape: per_image(shape) if len(shape) == 3 else resident(shape)
+    in_specs = [spec(arg.shape) for arg in args]
+    if core is not None:
+        in_specs = [pl.BlockSpec(memory_space=pltpu.SMEM)] + in_specs
+        args = (core,) + tuple(args)
     return pl.pallas_call(
         kernel,
         grid=(images,),
-        in_specs=[spec(arg.shape) for arg in args],
+        in_specs=in_specs,
         out_specs=[spec(out.shape) for out in outs],
         out_shape=outs,
-        compiler_params=pltpu.CompilerParams(vmem_limit_bytes=48 << 20),
+        compiler_params=pltpu.CompilerParams(vmem_limit_bytes=VMEM_BYTES),
         name=name,
     )(*args)
 
 
+def low_of(like, width):
+    return jax.ShapeDtypeStruct(like.shape[:2] + (width,), jnp.bfloat16)
+
+
+def total_of(rows, width):
+    return jax.ShapeDtypeStruct((rows, width), jnp.float32)
+
+
 def attention_forward(tokens, gain, bias, weight, proj_bias, out_mine, out_theirs):
-    images, rows, features = tokens.shape
-    struct = lambda width: jax.ShapeDtypeStruct((images, rows, width), jnp.bfloat16)
     half = out_mine.shape[1]
-    outs = [
-        struct(features),
-        struct(weight.shape[1]),
-        struct(out_mine.shape[0]),
-        struct(half),
-        struct(half),
-    ]
+    widths = (tokens.shape[2], weight.shape[1], out_mine.shape[0], half, half)
+    outs = [low_of(tokens, width) for width in widths]
     args = (tokens, gain, bias, weight, proj_bias, out_mine, out_theirs)
-    return run_images(forward_kernel, images, args, outs, "attention_forward")
-
-
-def attention_backward(packed, upstream, out_weight, back_mine, back_theirs):
-    images, rows, width = packed.shape
-    struct = lambda columns: jax.ShapeDtypeStruct((images, rows, columns), jnp.bfloat16)
-    sums = jax.ShapeDtypeStruct((1, width // 3), jnp.float32)
-    half = back_mine.shape[0]
-    outs = [struct(width), struct(half), struct(half), sums, sums]
-    args = (packed, upstream, out_weight, back_mine, back_theirs)
-    return run_images(backward_kernel, images, args, outs, "attention_backward")
+    return run_images(forward_kernel, args, outs, "attention_forward")
+
+
+def hidden_both(core, tokens, *args):
+    mine, up_weight = args[0], args[4]
+    features, units, half = tokens.shape[2], up_weight.shape[1], mine.shape[2]
+    widths = (features, features, units, features, units, half, half)
+    outs = [low_of(tokens, width) for width in widths] + [total_of(1, units)]
+    return run_images(hidden_kernel, (tokens,) + args, outs, "hidden_both", core)
+
+
+def attention_backward(core, tokens, *args):
+    packed, back_mine = args[5], args[7]
+    features, width, half = tokens.shape[2], packed.shape[2], back_mine.shape[0]
+    outs = [jax.ShapeDtypeStruct(tokens.shape, jnp.float32)]
+    outs += [low_of(tokens, columns) for columns in (features, width, half, half)]
+    outs += [total_of(1, width // 3), total_of(1, width // 3), total_of(4, features)]
+    return run_images(backward_kernel, (tokens,) + args, outs, "attention_backward", core)
 
 
 def exchange(block, axis, bit):
@@ -207,6 +270,12 @@
     odd = jnp.concatenate(blocks[1::2], axis=dim)
     upper = bit_of("tensor", 0)
     return jnp.where(upper, odd, even), jnp.where(upper, even, odd)
+
+
+def split_halves(values, dim):
+    low, high = jnp.split(values, 2, axis=dim)
+    upper = bit_of("tensor", 0)
+    return jnp.where(upper, high, low), jnp.where(upper, low, high)
 
 
 def join_blocks(mine, theirs):
@@ -336,10 +405,7 @@
 
     tokens = pad_rows(tokens)
     cotangent = pad_rows(cotangent)
-    out_mine, out_theirs = split_blocks(out_weight, 1)
-    qkv_mine, qkv_theirs = split_blocks(qkv_weight, 0)
-    up_mine, up_theirs = split_blocks(up_weight, 0)
-    down_mine, down_theirs = split_blocks(down_weight, 1)
+    core = (lax.axis_index("tensor") % 2).astype(jnp.int32).reshape(1)
     proj_bias = jnp.stack(
         [
             query_bias.reshape(heads_local, HD),
@@ -349,99 +415,85 @@
         axis=1,
     ).reshape(1, 3 * heads_local * HD)
     tokens_far = [gather_far(part) for part in in_chunks(tokens)]
-    scale2_all = gather_near(gather_far(layer_scale2[None]))
+    out_mine, out_theirs = split_halves(out_weight, 1)
     whole = [gather_near(part) for part in tokens_far]
     cotangent_far = gather_far(after(cotangent, *tokens_far))
-    upstream_low = gather_near(cotangent_far)
-
+    scale2_all = gather_near(gather_far(layer_scale2[None]))
     forward = [
         attention_forward(
             part, norm1_gain[None], norm1_bias[None], qkv_weight, proj_bias, out_mine, out_theirs
         )
         for part in whole
     ]
-    upstream = [flat(part) for part in in_chunks(upstream_low)]
-    branch_grad = [(part.astype(jnp.float32) * scale2_all).astype(jnp.bfloat16) for part in upstream]
-
-    attended_low, normed2, inv_std2, lowered2, residual = [], [], [], [], []
-    activated_low, grad_pre, grad_pre_low = [], [], []
+    upstream = in_chunks(gather_near(cotangent_far))
+    up_mine, up_theirs = split_halves(up_weight, 0)
+    vectors = jnp.concatenate(
+        [out_bias[None], layer_scale1[None], norm2_gain[None], norm2_bias[None], scale2_all]
+    )
+
+    hidden = []
     for index in range(chunks):
-        _, _, _, mine, theirs = forward[index]
-        total = add_far(add_near(flat(mine), flat(theirs)))
-        joined = gather_near(total)
-        attended_low.append(joined)
-        attended = joined.astype(jnp.float32) + out_bias
-        residual.append(flat(whole[index]).astype(jnp.float32) + layer_scale1 * attended)
-        normed, inv_std, scaled = layer_norm(residual[index], norm2_gain, norm2_bias)
-        normed2.append(normed)
-        inv_std2.append(inv_std)
-        lowered2.append(scaled.astype(jnp.bfloat16))
-        hidden_pre = (
-            jnp.dot(lowered2[index], up_weight, preferred_element_type=jnp.float32) + up_bias
-        )
-        activated, slope = gelu_parts(hidden_pre)
-        activated_low.append(activated.astype(jnp.bfloat16))
-        grad_pre.append(contract_cols(branch_grad[index], down_weight) * slope)
-        grad_pre_low.append(grad_pre[index].astype(jnp.bfloat16))
-
-    lowered2_all = out_of_chunks(lowered2)
-    activated_all = out_of_chunks(activated_low)
-    grad_pre_all = out_of_chunks(grad_pre_low)
-    branch_grad_all = out_of_chunks(branch_grad)
-    grad_down_weight = contract_rows(activated_all, branch_grad_all)
-    grad_up_weight = contract_rows(lowered2_all, grad_pre_all)
-    grad_up_bias = sum(jnp.sum(part, axis=0) for part in grad_pre)
-
-    grad_residual, grad_attended, sums2 = [], [], []
+        mine = add_far(add_near(*forward[index][3:5]))
+        theirs = exchange(mine, "tensor", 0)
+        hidden.append(
+            hidden_both(
+                core,
+                whole[index],
+                mine,
+                theirs,
+                upstream[index],
+                vectors,
+                up_weight,
+                up_bias[None],
+                down_weight,
+                up_mine,
+                up_theirs,
+            )
+        )
+    every = lambda index: flat(out_of_chunks([parts[index] for parts in hidden]))
+    activated_all = every(2)
+    grad_down_weight = contract_rows(activated_all, every(3))
+    grad_up_weight = contract_rows(every(1), every(4))
+    grad_up_bias = sum(parts[7] for parts in hidden)[0]
+
+    qkv_mine, qkv_theirs = split_blocks(qkv_weight, 0)
     back = []
     for index in range(chunks):
-        total = add_far(
-            add_near(
-                contract_cols(grad_pre_low[index], up_mine).astype(jnp.bfloat16),
-                contract_cols(grad_pre_low[index], up_theirs).astype(jnp.bfloat16),
-            )
-        )
-        grad_lowered2 = gather_near(total).astype(jnp.float32)
-        part = upstream[index].astype(jnp.float32) + norm_back(
-            grad_lowered2, normed2[index], inv_std2[index], norm2_gain
-        )
-        grad_residual.append(part)
-        attended = attended_low[index].astype(jnp.float32) + out_bias
-        sums2.append(
-            (
-                jnp.sum(grad_lowered2 * normed2[index], axis=0),
-                jnp.sum(grad_lowered2, axis=0),
-                jnp.sum(part * attended, axis=0),
-                jnp.sum(part * layer_scale1, axis=0),
-            )
-        )
-        grad_attended.append((part * layer_scale1).astype(jnp.bfloat16))
-        packed = forward[index][1]
+        mine = add_far(add_near(*hidden[index][5:7]))
+        theirs = exchange(mine, "tensor", 0)
         back.append(
             attention_backward(
-                packed,
-                grad_attended[index].reshape(packed.shape[:2] + (features,)),
+                core,
+                whole[index],
+                hidden[index][0],
+                mine,
+                theirs,
+                upstream[index],
+                vectors,
+                forward[index][1],
                 out_weight,
                 qkv_mine,
                 qkv_theirs,
             )
         )
-    grad_norm2_gain, grad_norm2_bias, grad_layer_scale1, grad_out_bias = (
-        sum(parts) for parts in zip(*sums2)
-    )
-    grad_query_bias = sum(parts[3] for parts in back)[0]
-    grad_value_bias = sum(parts[4] for parts in back)[0]
+    grad_norm2_gain, grad_norm2_bias, grad_layer_scale1, grad_out_bias = sum(
+        parts[7] for parts in back
+    )
+    grad_query_bias = sum(parts[5] for parts in back)[0]
+    grad_value_bias = sum(parts[6] for parts in back)[0]
     grad_out_weight = contract_rows(
-        flat(out_of_chunks([parts[2] for parts in forward])), out_of_chunks(grad_attended)
+        flat(out_of_chunks([parts[2] for parts in forward])),
+        flat(out_of_chunks([parts[1] for parts in back])),
     )
     grad_qkv_weight = contract_rows(
         flat(out_of_chunks([parts[0] for parts in forward])),
-        flat(out_of_chunks([parts[0] for parts in back])),
+        flat(out_of_chunks([parts[2] for parts in back])),
     )
     grad_lowered1 = out_of_chunks(
-        [scatter_far(add_near(flat(parts[1]), flat(parts[2]))) for parts in back]
-    )
-
+        [scatter_far(add_near(flat(parts[3]), flat(parts[4]))) for parts in back]
+    )
+
+    down_mine, down_theirs = split_blocks(down_weight, 1)
     branch_cols = (
         scatter_far(
             add_near(
@@ -455,7 +507,11 @@
         )
         + down_bias
     )
-    output = out_of_chunks([cols(part) for part in residual]) + layer_scale2 * branch_cols
+    attended_cols = flat(out_of_chunks([cols(parts[0]) for parts in hidden])).astype(jnp.float32)
+    residual_cols = flat(tokens).astype(jnp.float32) + cols(layer_scale1) * (
+        attended_cols + cols(out_bias)
+    )
+    output = residual_cols + layer_scale2 * branch_cols
     upstream_cols = flat(cotangent).astype(jnp.float32)
     grad_layer_scale2 = jnp.sum(upstream_cols * branch_cols, axis=0)
     grad_down_bias = jnp.sum(upstream_cols * layer_scale2, axis=0)
@@ -470,7 +526,7 @@
         [jnp.sum(scaled, axis=-1), jnp.sum(scaled * normed1_cols, axis=-1)], "tensor"
     )
     mean_scaled, mean_product = (values[:, None] / features for values in row_sums)
-    input_grad = out_of_chunks([cols(part) for part in grad_residual]) + inv_std1 * (
+    input_grad = flat(out_of_chunks([cols(parts[0]) for parts in back])) + inv_std1 * (
         scaled - mean_scaled - normed1_cols * mean_product
     )
 

time: 405 us -> 350 us (0.86)
  waiting for transfers between devices: 160 us -> 120 us
  other arithmetic: 89 us -> 57.3 us
  Pallas kernels: 26.2 us -> 52.6 us
  matrix products: 29.9 us -> 13.5 us
  starting transfers between devices: 60.8 us -> 74 us
  local copies, waits for them, and re-layouts: 31.5 us -> 25.5 us
    ppermute x66, waiting for transfers between devices: 160 us -> 120 us  [exchange(): lax.ppermute(block, axis, [(index, index ^ 1 << bit) for index in range(s...]
    pallas_call x4 -> x6, Pallas kernels: 26.2 us -> 52.6 us  [run_images(): pl.pallas_call(kernel, grid=(images,), in_specs=in_specs, out_specs=[spec...]
    reduce_sum x9 -> x0, other arithmetic: 20.2 us -> none  [the longest x2 5.07 us: layer_norm(): jnp.mean(centred * centred, axis=-1, keepdims=True) + EPS]
    dot_general x8 -> x0, matrix products: 15.9 us -> none  [the longest x6 11.5 us: contract_cols(): lax.dot_general(left, right, (((1,), (1,)), ((), ())), preferred_element_...]
    convert_element_type x4 -> x1, other arithmetic: 15.1 us -> 1.09 us  [shards(): flat(tokens).astype(jnp.float32)]
    ppermute x66, starting transfers between devices: 60.8 us -> 74 us  [exchange(): lax.ppermute(block, axis, [(index, index ^ 1 << bit) for index in range(s...]
    split x4 -> x2, local copies, waits for them, and re-layouts: 6.84 us -> 2.56 us  [split_blocks(): blocks = jnp.split(values, count, axis=dim)]
    unnamed x337 -> x165, local copies, waits for them, and re-layouts: 8.27 us -> 5.49 us
  transfers between devices with their start and end apart: 66 -> 66, of which waited for: 28 -> 25; matrix products, arithmetic and copies ran while one was open for 25% -> 26% of each run, Pallas kernels for 7% -> 15%
where the time goes in v3:
time: 350 us; the launch traced here: 346 us
  waiting for transfers between devices  120 us (34%)
  starting transfers between devices  74 us (21%)
  other arithmetic  57.3 us (16%)
  Pallas kernels  52.6 us (15%)
  local copies, waits for them, and re-layouts  25.5 us (7%)
  matrix products  13.5 us (4%)
    ppermute x66, waiting for transfers between devices, exchange(): lax.ppermute(block, axis, [(index, index ^ 1 << bit) for index in range(s...  120 us
    ppermute x66, starting transfers between devices, exchange(): lax.ppermute(block, axis, [(index, index ^ 1 << bit) for index in range(s...  74 us
    pallas_call x6, Pallas kernels, run_images(): pl.pallas_call(kernel, grid=(images,), in_specs=in_specs, out_specs=[spec...  52.6 us
    dot_general x4, matrix products, contract_rows(): lax.dot_general(left, right, (((0,), (0,)), ((), ())), preferred_element_...  9.14 us
    select_n x15, other arithmetic, double_rows(): jnp.where(upper, got, grad)  7.32 us
  transfers between devices with their start and end apart: 66, of which 25 were waited for; matrix products, arithmetic and copies ran while one was open for 26% of the time, Pallas kernels for 15%

profile of v3, /device:TPU:0, one launch (start us, length us, event | category | flops | bytes accessed | tf_op | source)
XLA Modules:
  0.0 346.1 jit_solution(10943123732092794499)
XLA Ops:
  0.7 3.0 collective-permute-start.8
  11.1 2.7 broadcast_select_fusion.6
  19.7 4.6 %collective-permute-done.5 = bf16[2,264,256]{2,1,0:T(8,128)(2,1)S(1)} collective-permute-done((bf16[2,264,256]{2,1,0:T(8,128)(2,1)S(1)}, bf16[2,264,256]{2,1,0:T(8,128)(2,1)S(1)}, u32[]{:S(2)}, u32[]{:S(2)}) %collective-permute-start.5) | collective-permute-done | bytes 270368 | tf_op jit(solution)/shard_map/ppermute | solution.py:251
  28.7 7.1 %attention_forward.2 = (bf16[2,264,1024]{2,1,0:T(8,128)(2,1)S(1)}, bf16[2,264,768]{2,1,0:T(8,128)(2,1)S(1)}, bf16[2,264,256]{2,1,0:T(8,128)(2,1)S(1)}, bf16[2,26...) custom-call(bf16[2,264,1024]{2,1,0:T(8,128)(2,1)S(1)} %pad_maximum_fusion.2.tokens, f32[1,1024]{1,0:T(1,128)S(1)} %bitcast.56, ...), custom_call_target="tpu_custom_call" | custom-call | tf_op jit(solution)/shard_map/attention_forward/pallas_call | solution.py:205
  37.4 7.0 %attention_forward.3 = (bf16[2,264,1024]{2,1,0:T(8,128)(2,1)S(1)}, bf16[2,264,768]{2,1,0:T(8,128)(2,1)S(1)}, bf16[2,264,256]{2,1,0:T(8,128)(2,1)S(1)}, bf16[2,26...) custom-call(bf16[2,264,1024]{2,1,0:T(8,128)(2,1)S(1)} %pad_maximum_fusion.4.tokens, f32[1,1024]{1,0:T(1,128)S(1)} %bitcast.57, ...), custom_call_target="tpu_custom_call" | custom-call | tf_op jit(solution)/shard_map/attention_forward/pallas_call | solution.py:205
  51.7 12.1 %collective-permute-done.3 = bf16[2,264,512]{2,1,0:T(8,128)(2,1)S(1)} collective-permute-done((bf16[2,264,512]{2,1,0:T(8,128)(2,1)S(1)}, bf16[2,264,512]{2,1,0:T(8,128)(2,1)S(1)}, u32[]{:S(2)}, u32[]{:S(2)}) %collective-permute-start.3) | collective-permute-done | bytes 540704 | tf_op jit(solution)/shard_map/ppermute | solution.py:251
  64.0 10.7 %collective-permute-done.12 = bf16[2,264,512]{2,1,0:T(8,128)(2,1)S(1)} collective-permute-done((bf16[2,264,512]{2,1,0:T(8,128)(2,1)S(1)}, bf16[2,264,512]{2,1,0:T(8,128)(2,1)S(1)}, u32[]{:S(2)}, u32[]{:S(2)}) %collective-permute-start.12) | collective-permute-done | bytes 540704 | tf_op jit(solution)/shard_map/ppermute | solution.py:251
  77.0 8.3 %hidden_both.2 = (bf16[2,264,1024]{2,1,0:T(8,128)(2,1)S(1)}, bf16[2,264,1024]{2,1,0:T(8,128)(2,1)}, bf16[2,264,1024]{2,1,0:T(8,128)(2,1)}, bf16[2,264,1024]{2,1,...) custom-call(s32[1]{0:T(128)} %bitcast.1.core, ...), custom_call_target="tpu_custom_call" | custom-call | tf_op jit(solution)/shard_map/hidden_both/pallas_call | solution.py:205
  88.2 8.4 %hidden_both.3 = (bf16[2,264,1024]{2,1,0:T(8,128)(2,1)S(1)}, bf16[2,264,1024]{2,1,0:T(8,128)(2,1)}, bf16[2,264,1024]{2,1,0:T(8,128)(2,1)}, bf16[2,264,1024]{2,1,...) custom-call(s32[1]{0:T(128)} %bitcast.1.core, ...), custom_call_target="tpu_custom_call" | custom-call | tf_op jit(solution)/shard_map/hidden_both/pallas_call | solution.py:205
  97.1 2.9 constant_dynamic-update-slice_fusion
  100.0 3.1 convolution_convert_fusion
  103.3 3.0 fusion.23
  108.1 2.9 fusion.26
  116.3 10.2 %collective-permute-done.17 = bf16[2,264,512]{2,1,0:T(8,128)(2,1)S(1)} collective-permute-done((bf16[2,264,512]{2,1,0:T(8,128)(2,1)S(1)}, bf16[2,264,512]{2,1,0:T(8,128)(2,1)S(1)}, u32[]{:S(2)}, u32[]{:S(2)}) %collective-permute-start.17) | collective-permute-done | bytes 540704 | tf_op jit(solution)/shard_map/ppermute | solution.py:251
  126.7 5.3 %collective-permute-done.60 = bf16[512,1024]{1,0:T(8,128)(2,1)S(1)} collective-permute-done((bf16[512,1024]{1,0:T(8,128)(2,1)S(1)}, bf16[512,1024]{1,0:T(8,128)(2,1)S(1)}, u32[]{:S(2)}, u32[]{:S(2)}) %collective-permute-start.60) | collective-permute-done | bytes 1048608 | tf_op jit(solution)/shard_map/ppermute | solution.py:251
  135.1 3.0 collective-permute-done.54
  144.8 10.9 %attention_backward.2 = (f32[2,264,1024]{2,1,0:T(8,128)}, bf16[2,264,1024]{2,1,0:T(8,128)(2,1)}, bf16[2,264,768]{2,1,0:T(8,128)(2,1)S(1)}, bf16[2,264,512]{2,1,0...) custom-call(s32[1]{0:T(128)} %bitcast.1.core, ...), custom_call_target="tpu_custom_call" | custom-call | tf_op jit(solution)/shard_map/attention_backward/pallas_call | solution.py:205
  160.0 2.6 collective-permute-start.62
  165.1 10.9 %attention_backward.3 = (f32[2,264,1024]{2,1,0:T(8,128)}, bf16[2,264,1024]{2,1,0:T(8,128)(2,1)}, bf16[2,264,768]{2,1,0:T(8,128)(2,1)S(1)}, bf16[2,264,512]{2,1,0...) custom-call(s32[1]{0:T(128)} %bitcast.1.core, ...), custom_call_target="tpu_custom_call" | custom-call | tf_op jit(solution)/shard_map/attention_backward/pallas_call | solution.py:205
  181.6 2.6 fusion.46
  191.9 2.6 collective-permute-start.47
  211.7 9.4 %collective-permute-done.49 = bf16[64,1024]{1,0:T(8,128)(2,1)S(1)} collective-permute-done((bf16[64,1024]{1,0:T(8,128)(2,1)S(1)}, bf16[64,1024]{1,0:T(8,128)(2,1)S(1)}, u32[]{:S(2)}, u32[]{:S(2)}) %collective-permute-start.49) | collective-permute-done | bytes 131104 | tf_op jit(solution)/shard_map/ppermute | solution.py:251
  222.3 2.9 collective-permute-start.50
  225.6 9.0 %collective-permute-done.50 = bf16[32,1024]{1,0:T(8,128)(2,1)S(1)} collective-permute-done((bf16[32,1024]{1,0:T(8,128)(2,1)S(1)}, bf16[32,1024]{1,0:T(8,128)(2,1)S(1)}, u32[]{:S(2)}, u32[]{:S(2)}) %collective-permute-start.50) | collective-permute-done | bytes 65568 | tf_op jit(solution)/shard_map/ppermute | solution.py:251
  250.1 8.1 %collective-permute-done.52 = bf16[64,1024]{1,0:T(8,128)(2,1)S(1)} collective-permute-done((bf16[64,1024]{1,0:T(8,128)(2,1)S(1)}, bf16[64,1024]{1,0:T(8,128)(2,1)S(1)}, u32[]{:S(2)}, u32[]{:S(2)}) %collective-permute-start.52) | collective-permute-done | bytes 131104 | tf_op jit(solution)/shard_map/ppermute | solution.py:251
  263.7 2.9 collective-permute-start.42
  266.6 2.6 collective-permute-done.42
  269.3 3.5 %collective-permute-start.36 = (bf16[64,768]{1,0:T(8,128)(2,1)S(1)}, bf16[64,768]{1,0:T(8,128)(2,1)S(1)}, u32[]{:S(2)}, u32[]{:S(2)}) collective-permute-start(bf16[64,768]{1,0:T(8,128)(2,1)S(1)} %add_convert_fusion.11), channel_id=1, source_target_pairs={{0,16},{4,20},{8,24},{12,28},{16,0},{20,4},{24,8},{28,12},{1,17},{... | collective-permute-start | bytes 294920 | tf_op jit(solution)/shard_map/ppermute | solution.py:251
  279.5 3.5 %collective-permute-start.29 = (f32[512]{0:T(512)S(1)}, f32[512]{0:T(512)S(1)}, u32[]{:S(2)}, u32[]{:S(2)}) collective-permute-start(f32[512]{0:T(512)S(1)} %fusion.60), channel_id=1, source_target_pairs={{0,8},{4,12},{8,0},{12,4},{16,24},{20,28},{24,16},{28,20},{1,9},{5... | collective-permute-start | bytes 6152 | tf_op jit(solution)/shard_map/ppermute | solution.py:251
  285.4 3.7 %collective-permute-done.30 = f32[512]{0:T(512)S(1)} collective-permute-done((f32[512]{0:T(512)S(1)}, f32[512]{0:T(512)S(1)}, u32[]{:S(2)}, u32[]{:S(2)}) %collective-permute-start.30) | collective-permute-done | bytes 2080 | tf_op jit(solution)/shard_map/ppermute | solution.py:251
  315.4 4.0 %collective-permute-done.44 = bf16[256,768]{1,0:T(8,128)(2,1)S(1)} collective-permute-done((bf16[256,768]{1,0:T(8,128)(2,1)S(1)}, bf16[256,768]{1,0:T(8,128)(2,1)S(1)}, u32[]{:S(2)}, u32[]{:S(2)}) %collective-permute-start.44) | collective-permute-done | bytes 393248 | tf_op jit(solution)/shard_map/ppermute | solution.py:251
  322.6 17.0 %collective-permute-done.59 = bf16[512,1024]{1,0:T(8,128)(2,1)S(1)} collective-permute-done((bf16[512,1024]{1,0:T(8,128)(2,1)S(1)}, bf16[512,1024]{1,0:T(8,128)(2,1)S(1)}, u32[]{:S(2)}, u32[]{:S(2)}) %collective-permute-start.59) | collective-permute-done | bytes 1048608 | tf_op jit(solution)/shard_map/ppermute | solution.py:251
  (433 shorter events, 153.1 us)
Async XLA Ops:
  0.7 17.5 %collective-permute-start.8 = (f32[1,256]{1,0:T(1,128)}, f32[1,256]{1,0:T(1,128)S(1)}, u32[]{:S(2)}, u32[]{:S(2)}) collective-permute-start(f32[1,256]{1,0:T(1,128)} %bitcast.74), channel_id=1, source_target_pairs={{0,2},{1,3},{2,0},{3,1},{4,6},{5,7},{6,4},{7,5},{8,10},{9,11},{10,... | collective-permute-start | bytes 3080 | tf_op jit(solution)/shard_map/ppermute | solution.py:251
  25.5 21.5 %collective-permute-start.6 = (bf16[4,264,256]{2,1,0:T(8,128)(2,1)}, bf16[4,264,256]{2,1,0:T(8,128)(2,1)}, u32[]{:S(2)}, u32[]{:S(2)}) collective-permute-start(bf16[4,264,256]{2,1,0:T(8,128)(2,1)} %pad.8), channel_id=1, source_target_pairs={{0,2},{1,3},{2,0},{3,1},{4,6},{5,7},{6,4},{7,5},{8,10},{9,11},{10,... | collective-permute-start | bytes 1622024 | tf_op jit(solution)/shard_map/ppermute | solution.py:251
  48.2 26.8 %collective-permute-start.7 = (bf16[4,264,512]{2,1,0:T(8,128)(2,1)S(1)}, bf16[4,264,512]{2,1,0:T(8,128)(2,1)S(1)}, u32[]{:S(2)}, u32[]{:S(2)}) collective-permute-start(bf16[4,264,512]{2,1,0:T(8,128)(2,1)S(1)} %pad_maximum_fusion.3), channel_id=1, source_target_pairs={{0,1},{1,0},{2,3},{3,2},{4,5},{5,4},{6,7},{7,6},{8,9},{9,8},{10,11... | collective-permute-start | bytes 3244040 | tf_op jit(solution)/shard_map/ppermute | solution.py:251
  49.3 25.5 %collective-permute-start.12 = (bf16[2,264,512]{2,1,0:T(8,128)(2,1)S(1)}, bf16[2,264,512]{2,1,0:T(8,128)(2,1)S(1)}, u32[]{:S(2)}, u32[]{:S(2)}) collective-permute-start(bf16[2,264,512]{2,1,0:T(8,128)(2,1)S(1)} %add_convert_fusion.5), channel_id=1, source_target_pairs={{0,2},{1,3},{2,0},{3,1},{4,6},{5,7},{6,4},{7,5},{8,10},{9,11},{10,... | collective-permute-start | bytes 1622024 | tf_op jit(solution)/shard_map/ppermute | solution.py:251
  85.3 25.8 %collective-permute-start.16 = (bf16[2,264,512]{2,1,0:T(8,128)(2,1)S(1)}, bf16[2,264,512]{2,1,0:T(8,128)(2,1)S(1)}, u32[]{:S(2)}, u32[]{:S(2)}) collective-permute-start(bf16[2,264,512]{2,1,0:T(8,128)(2,1)S(1)} %get-tuple-element.70), channel_id=1, source_target_pairs={{0,1},{1,0},{2,3},{3,2},{4,5},{5,4},{6,7},{7,6},{8,9},{9,8},{10,11... | collective-permute-start | bytes 1622024 | tf_op jit(solution)/shard_map/ppermute | solution.py:251
  96.7 17.9 %collective-permute-start.19 = (bf16[2,264,512]{2,1,0:T(8,128)(2,1)S(1)}, bf16[2,264,512]{2,1,0:T(8,128)(2,1)S(1)}, u32[]{:S(2)}, u32[]{:S(2)}) collective-permute-start(bf16[2,264,512]{2,1,0:T(8,128)(2,1)S(1)} %get-tuple-element.74), channel_id=1, source_target_pairs={{0,1},{1,0},{2,3},{3,2},{4,5},{5,4},{6,7},{7,6},{8,9},{9,8},{10,11... | collective-permute-start | bytes 1622024 | tf_op jit(solution)/shard_map/ppermute | solution.py:251
  103.1 38.0 %collective-permute-start.14 = (bf16[1056,512]{1,0:T(8,128)(2,1)S(1)}, bf16[1056,512]{1,0:T(8,128)(2,1)S(1)}, u32[]{:S(2)}, u32[]{:S(2)}) collective-permute-start(bf16[1056,512]{1,0:T(8,128)(2,1)S(1)} %convolution_convert_fusion), channel_id=1, source_target_pairs={{0,1},{1,0},{2,3},{3,2},{4,5},{5,4},{6,7},{7,6},{8,9},{9,8},{10,11... | collective-permute-start | bytes 3244040 | tf_op jit(solution)/shard_map/ppermute | solution.py:251
  106.5 25.5 %collective-permute-start.60 = (bf16[512,1024]{1,0:T(8,128)(2,1)S(1)}, bf16[512,1024]{1,0:T(8,128)(2,1)S(1)}, u32[]{:S(2)}, u32[]{:S(2)}) collective-permute-start(bf16[512,1024]{1,0:T(8,128)(2,1)S(1)} %select_convert_fusion), channel_id=1, source_target_pairs={{0,4},{4,0},{8,12},{12,8},{16,20},{20,16},{24,28},{28,24},{1,5},{5... | collective-permute-start | bytes 3145736 | tf_op jit(solution)/shard_map/ppermute | solution.py:251
  111.2 15.2 %collective-permute-start.17 = (bf16[2,264,512]{2,1,0:T(8,128)(2,1)S(1)}, bf16[2,264,512]{2,1,0:T(8,128)(2,1)S(1)}, u32[]{:S(2)}, u32[]{:S(2)}) collective-permute-start(bf16[2,264,512]{2,1,0:T(8,128)(2,1)S(1)} %add_convert_fusion.3), channel_id=1, source_target_pairs={{0,2},{1,3},{2,0},{3,1},{4,6},{5,7},{6,4},{7,5},{8,10},{9,11},{10,... | collective-permute-start | bytes 1622024 | tf_op jit(solution)/shard_map/ppermute | solution.py:251
  112.1 26.0 %collective-permute-start.54 = (bf16[512,1024]{1,0:T(8,128)(2,1)S(1)}, bf16[512,1024]{1,0:T(8,128)(2,1)S(1)}, u32[]{:S(2)}, u32[]{:S(2)}) collective-permute-start(bf16[512,1024]{1,0:T(8,128)(2,1)S(1)} %select_convert_fusion.1), channel_id=1, source_target_pairs={{0,8},{4,12},{8,0},{12,4},{16,24},{20,28},{24,16},{28,20},{1,9},{5... | collective-permute-start | bytes 3145736 | tf_op jit(solution)/shard_map/ppermute | solution.py:251
  114.7 26.1 %collective-permute-start.20 = (bf16[2,264,512]{2,1,0:T(8,128)(2,1)S(1)}, bf16[2,264,512]{2,1,0:T(8,128)(2,1)S(1)}, u32[]{:S(2)}, u32[]{:S(2)}) collective-permute-start(bf16[2,264,512]{2,1,0:T(8,128)(2,1)S(1)} %add_convert_fusion.1), channel_id=1, source_target_pairs={{0,2},{1,3},{2,0},{3,1},{4,6},{5,7},{6,4},{7,5},{8,10},{9,11},{10,... | collective-permute-start | bytes 1622024 | tf_op jit(solution)/shard_map/ppermute | solution.py:251
  126.6 18.2 %collective-permute-start.18 = (bf16[2,264,512]{2,1,0:T(8,128)(2,1)S(1)}, bf16[2,264,512]{2,1,0:T(8,128)(2,1)S(1)}, u32[]{:S(2)}, u32[]{:S(2)}) collective-permute-start(bf16[2,264,512]{2,1,0:T(8,128)(2,1)S(1)} %add_convert_fusion.2.low2_mine), channel_id=1, source_target_pairs={{0,1},{1,0},{2,3},{3,2},{4,5},{5,4},{6,7},{7,6},{8,9},{9,8},{10,11... | collective-permute-start | bytes 1622024 | tf_op jit(solution)/shard_map/ppermute | solution.py:251
  133.5 24.4 %collective-permute-start.61 = (bf16[256,1024]{1,0:T(8,128)(2,1)}, bf16[256,1024]{1,0:T(8,128)(2,1)}, u32[]{:S(2)}, u32[]{:S(2)}) collective-permute-start(bf16[256,1024]{1,0:T(8,128)(2,1)} %select_convert_fusion.3), channel_id=1, source_target_pairs={{0,8},{4,12},{8,0},{12,4},{16,24},{20,28},{24,16},{28,20},{1,9},{5... | collective-permute-start | bytes 1572872 | tf_op jit(solution)/shard_map/ppermute | solution.py:251
  139.5 23.1 %collective-permute-start.55 = (bf16[256,1024]{1,0:T(8,128)(2,1)}, bf16[256,1024]{1,0:T(8,128)(2,1)}, u32[]{:S(2)}, u32[]{:S(2)}) collective-permute-start(bf16[256,1024]{1,0:T(8,128)(2,1)} %select_convert_fusion.4), channel_id=1, source_target_pairs={{0,4},{4,0},{8,12},{12,8},{16,20},{20,16},{24,28},{28,24},{1,5},{5... | collective-permute-start | bytes 1572872 | tf_op jit(solution)/shard_map/ppermute | solution.py:251
  141.0 24.1 %collective-permute-start.21 = (bf16[2,264,512]{2,1,0:T(8,128)(2,1)S(1)}, bf16[2,264,512]{2,1,0:T(8,128)(2,1)S(1)}, u32[]{:S(2)}, u32[]{:S(2)}) collective-permute-start(bf16[2,264,512]{2,1,0:T(8,128)(2,1)S(1)} %add_convert_fusion.low2_mine), channel_id=1, source_target_pairs={{0,1},{1,0},{2,3},{3,2},{4,5},{5,4},{6,7},{7,6},{8,9},{9,8},{10,11... | collective-permute-start | bytes 1622024 | tf_op jit(solution)/shard_map/ppermute | solution.py:251
  143.4 36.3 %collective-permute-start.15 = (bf16[1056,256]{1,0:T(8,128)(2,1)}, bf16[1056,256]{1,0:T(8,128)(2,1)}, u32[]{:S(2)}, u32[]{:S(2)}) collective-permute-start(bf16[1056,256]{1,0:T(8,128)(2,1)} %select_convert_fusion.2), channel_id=1, source_target_pairs={{0,2},{1,3},{2,0},{3,1},{4,6},{5,7},{6,4},{7,5},{8,10},{9,11},{10,... | collective-permute-start | bytes 1622024 | tf_op jit(solution)/shard_map/ppermute | solution.py:251
  155.7 52.9 %collective-permute-start.22 = (bf16[528,512]{1,0:T(8,128)(2,1)}, bf16[528,512]{1,0:T(8,128)(2,1)}, u32[]{:S(2)}, u32[]{:S(2)}) collective-permute-start(bf16[528,512]{1,0:T(8,128)(2,1)} %bitcast.14), channel_id=1, source_target_pairs={{0,1},{1,0},{2,3},{3,2},{4,5},{5,4},{6,7},{7,6},{8,9},{9,8},{10,11... | collective-permute-start | bytes 1622024 | tf_op jit(solution)/shard_map/ppermute | solution.py:251
  160.0 40.8 %collective-permute-start.62 = (bf16[128,1024]{1,0:T(8,128)(2,1)}, bf16[128,1024]{1,0:T(8,128)(2,1)}, u32[]{:S(2)}, u32[]{:S(2)}) collective-permute-start(bf16[128,1024]{1,0:T(8,128)(2,1)} %select_convert_fusion.9), channel_id=1, source_target_pairs={{0,16},{4,20},{8,24},{12,28},{16,0},{20,4},{24,8},{28,12},{1,17},{... | collective-permute-start | bytes 786440 | tf_op jit(solution)/shard_map/ppermute | solution.py:251
  164.8 38.4 %collective-permute-start.56 = (bf16[128,1024]{1,0:T(8,128)(2,1)}, bf16[128,1024]{1,0:T(8,128)(2,1)}, u32[]{:S(2)}, u32[]{:S(2)}) collective-permute-start(bf16[128,1024]{1,0:T(8,128)(2,1)} %select_convert_fusion.10), channel_id=1, source_target_pairs={{0,16},{4,20},{8,24},{12,28},{16,0},{20,4},{24,8},{28,12},{1,17},{... | collective-permute-start | bytes 786440 | tf_op jit(solution)/shard_map/ppermute | solution.py:251
  176.0 69.1 %collective-permute-start.24 = (bf16[528,512]{1,0:T(8,128)(2,1)}, bf16[528,512]{1,0:T(8,128)(2,1)}, u32[]{:S(2)}, u32[]{:S(2)}) collective-permute-start(bf16[528,512]{1,0:T(8,128)(2,1)} %bitcast.16), channel_id=1, source_target_pairs={{0,1},{1,0},{2,3},{3,2},{4,5},{5,4},{6,7},{7,6},{8,9},{9,8},{10,11... | collective-permute-start | bytes 1622024 | tf_op jit(solution)/shard_map/ppermute | solution.py:251
  200.8 20.3 %collective-permute-start.33 = (bf16[256,768]{1,0:T(8,128)(2,1)}, bf16[256,768]{1,0:T(8,128)(2,1)S(1)}, u32[]{:S(2)}, u32[]{:S(2)}) collective-permute-start(bf16[256,768]{1,0:T(8,128)(2,1)} %get-tuple-element.114), channel_id=1, source_target_pairs={{0,4},{4,0},{8,12},{12,8},{16,20},{20,16},{24,28},{28,24},{1,5},{5... | collective-permute-start | bytes 1179656 | tf_op jit(solution)/shard_map/ppermute | solution.py:251
  203.1 19.2 %collective-permute-start.39 = (bf16[256,768]{1,0:T(8,128)(2,1)}, bf16[256,768]{1,0:T(8,128)(2,1)S(1)}, u32[]{:S(2)}, u32[]{:S(2)}) collective-permute-start(bf16[256,768]{1,0:T(8,128)(2,1)} %get-tuple-element.115), channel_id=1, source_target_pairs={{0,8},{4,12},{8,0},{12,4},{16,24},{20,28},{24,16},{28,20},{1,9},{5... | collective-permute-start | bytes 1179656 | tf_op jit(solution)/shard_map/ppermute | solution.py:251
  208.1 27.3 %collective-permute-start.63 = (bf16[128,1024]{1,0:T(8,128)(2,1)S(1)}, bf16[128,1024]{1,0:T(8,128)(2,1)S(1)}, u32[]{:S(2)}, u32[]{:S(2)}) collective-permute-start(bf16[128,1024]{1,0:T(8,128)(2,1)S(1)} %add_convert_fusion.8), channel_id=1, source_target_pairs={{0,16},{4,20},{8,24},{12,28},{16,0},{20,4},{24,8},{28,12},{1,17},{... | collective-permute-start | bytes 786440 | tf_op jit(solution)/shard_map/ppermute | solution.py:251
  221.1 15.3 %collective-permute-start.57 = (bf16[128,1024]{1,0:T(8,128)(2,1)S(1)}, bf16[128,1024]{1,0:T(8,128)(2,1)S(1)}, u32[]{:S(2)}, u32[]{:S(2)}) collective-permute-start(bf16[128,1024]{1,0:T(8,128)(2,1)S(1)} %add_convert_fusion.9), channel_id=1, source_target_pairs={{0,16},{4,20},{8,24},{12,28},{16,0},{20,4},{24,8},{28,12},{1,17},{... | collective-permute-start | bytes 786440 | tf_op jit(solution)/shard_map/ppermute | solution.py:251
  221.2 22.4 %collective-permute-start.23 = (bf16[528,256]{1,0:T(8,128)(2,1)S(1)}, bf16[528,256]{1,0:T(8,128)(2,1)S(1)}, u32[]{:S(2)}, u32[]{:S(2)}) collective-permute-start(bf16[528,256]{1,0:T(8,128)(2,1)S(1)} %select_convert_fusion.8), channel_id=1, source_target_pairs={{0,2},{1,3},{2,0},{3,1},{4,6},{5,7},{6,4},{7,5},{8,10},{9,11},{10,... | collective-permute-start | bytes 811016 | tf_op jit(solution)/shard_map/ppermute | solution.py:251
  241.7 71.1 %collective-permute-start.64 = (bf16[256,1024]{1,0:T(8,128)(2,1)}, bf16[256,1024]{1,0:T(8,128)(2,1)}, u32[]{:S(2)}, u32[]{:S(2)}) collective-permute-start(bf16[256,1024]{1,0:T(8,128)(2,1)} %pad_maximum_fusion.20), channel_id=1, source_target_pairs={{0,8},{4,12},{8,0},{12,4},{16,24},{20,28},{24,16},{28,20},{1,9},{5... | collective-permute-start | bytes 1572872 | tf_op jit(solution)/shard_map/ppermute | solution.py:251
  243.6 65.7 %collective-permute-start.58 = (bf16[256,1024]{1,0:T(8,128)(2,1)}, bf16[256,1024]{1,0:T(8,128)(2,1)}, u32[]{:S(2)}, u32[]{:S(2)}) collective-permute-start(bf16[256,1024]{1,0:T(8,128)(2,1)} %pad_maximum_fusion.19), channel_id=1, source_target_pairs={{0,4},{4,0},{8,12},{12,8},{16,20},{20,16},{24,28},{28,24},{1,5},{5... | collective-permute-start | bytes 1572872 | tf_op jit(solution)/shard_map/ppermute | solution.py:251
  246.6 26.3 %collective-permute-start.25 = (bf16[528,256]{1,0:T(8,128)(2,1)S(1)}, bf16[528,256]{1,0:T(8,128)(2,1)S(1)}, u32[]{:S(2)}, u32[]{:S(2)}) collective-permute-start(bf16[528,256]{1,0:T(8,128)(2,1)S(1)} %select_convert_fusion.7), channel_id=1, source_target_pairs={{0,2},{1,3},{2,0},{3,1},{4,6},{5,7},{6,4},{7,5},{8,10},{9,11},{10,... | collective-permute-start | bytes 811016 | tf_op jit(solution)/shard_map/ppermute | solution.py:251
  261.1 42.9 %collective-permute-start.53 = (bf16[128,1024]{1,0:T(8,128)(2,1)}, bf16[128,1024]{1,0:T(8,128)(2,1)}, u32[]{:S(2)}, u32[]{:S(2)}) collective-permute-start(bf16[128,1024]{1,0:T(8,128)(2,1)} %pad_maximum_fusion.23), channel_id=1, source_target_pairs={{0,4},{4,0},{8,12},{12,8},{16,20},{20,16},{24,28},{28,24},{1,5},{5... | collective-permute-start | bytes 786440 | tf_op jit(solution)/shard_map/ppermute | solution.py:251
  278.3 27.9 %collective-permute-start.43 = (bf16[128,768]{1,0:T(8,128)(2,1)}, bf16[128,768]{1,0:T(8,128)(2,1)}, u32[]{:S(2)}, u32[]{:S(2)}) collective-permute-start(bf16[128,768]{1,0:T(8,128)(2,1)} %pad_maximum_fusion.25), channel_id=1, source_target_pairs={{0,4},{4,0},{8,12},{12,8},{16,20},{20,16},{24,28},{28,24},{1,5},{5... | collective-permute-start | bytes 589832 | tf_op jit(solution)/shard_map/ppermute | solution.py:251
  310.7 28.9 %collective-permute-start.59 = (bf16[512,1024]{1,0:T(8,128)(2,1)S(1)}, bf16[512,1024]{1,0:T(8,128)(2,1)S(1)}, u32[]{:S(2)}, u32[]{:S(2)}) collective-permute-start(bf16[512,1024]{1,0:T(8,128)(2,1)S(1)} %pad_maximum_fusion.8), channel_id=1, source_target_pairs={{0,8},{4,12},{8,0},{12,4},{16,24},{20,28},{24,16},{28,20},{1,9},{5... | collective-permute-start | bytes 3145736 | tf_op jit(solution)/shard_map/ppermute | solution.py:251
  314.1 28.5 %collective-permute-start.65 = (bf16[512,1024]{1,0:T(8,128)(2,1)S(1)}, bf16[512,1024]{1,0:T(8,128)(2,1)S(1)}, u32[]{:S(2)}, u32[]{:S(2)}) collective-permute-start(bf16[512,1024]{1,0:T(8,128)(2,1)S(1)} %pad_maximum_fusion.9), channel_id=1, source_target_pairs={{0,4},{4,0},{8,12},{12,8},{16,20},{20,16},{24,28},{28,24},{1,5},{5... | collective-permute-start | bytes 3145736 | tf_op jit(solution)/shard_map/ppermute | solution.py:251
  (112 other events, 710.7 us)
